TPU v7x, 32 devices: a whole 2x2x4 slice. The times are simulated.
32 devices in a mesh: stack: 2 (over x), scene: 16 (over z, y, core).
Axes of the slice: x: 2, y: 2, z: 4, core: 2. Of those that a mesh axis runs over, the one named last changes fastest.
Arguments:
- raw_echoes: bfloat16 [4096, 2, 4, 512], P('scene', None, 'stack'), parts along dimension 2, may hold values from -6 to 6
- azimuth_phase: float32 [8192, 512], P('stack', 'scene'), parts along dimension 0, may hold values from -3.140625 to 3.140625
- band_offset: int32 [1024], P(('stack', 'scene')), parts along dimension 0, may hold values from 0 to 8, as said below
- partners: int32 [2, 2], P('stack'), parts along dimension 0, may hold values from 0 to 0, as said below
Outputs:
- goldstein: bfloat16 [4, 1024, 2, 512], P('stack', None, None, 'scene'), parts along dimension 0
There are 2 independent parts, one for each index of `stack`. A program takes and returns all parts, laid end to end along the dimension named above; each array names one. Nothing has to cross between parts.
Inputs may be any that keep to these rules, and one draw needn't show every extreme that they name: `partners`: row i names two dates that precede date i + 1, each from 0 to i, possibly equal; the last row's first entry is 0. `band_offset`: both 0 and 8 occur among the range bins.
All inputs are finite; a program needn't handle non-finite values.
Results may differ from a plain program's by a relative error of at most 0.023.
Values may be sent and summed in bfloat16 or wider, within the bound.
A program may use at most 128 MiB of HBM per device.

v0:
```python
import math

import jax
import jax.numpy as jnp
import numpy as np
from jax import lax
from jax.experimental import pallas as pl
from jax.experimental.pallas import tpu as pltpu
from jax.sharding import PartitionSpec as P

SPLIT = 64
LOOKS = 4
PATCH = 64
SHIFT = 8
TAPS = 2 * SHIFT - 1
EPSILON = 1e-06
STRIP = 32
GROUPS = STRIP // 2
LANES = 2 * SPLIT
CHUNKS = STRIP // 4
HALO_CHUNKS = CHUNKS // 2
TABLES = 13
VMEM_LIMIT = 56 * 1024 * 1024


def base_tables():
    k = np.arange(64)
    angle = 2.0 * np.pi * ((k[:, None] * k[None, :]) % 64) / 64.0
    return np.cos(angle), np.sin(angle)


def twiddle_tables():
    k = np.arange(SPLIT)
    angle = 2.0 * np.pi * ((k[:, None] * k[None, :]) % (SPLIT * SPLIT)) / (SPLIT * SPLIT)
    return (
        np.tile(np.cos(angle), (1, 2)).astype(np.float32),
        np.tile(np.sin(angle), (1, 2)).astype(np.float32),
    )


def bf16(table):
    return jnp.asarray(np.asarray(table, np.float32), jnp.bfloat16)


def left_table(direction):
    c, s = base_tables()
    return np.block([[c, direction * s], [-direction * s, c]])


def right_table(direction):
    c, s = base_tables()
    eye = np.eye(2)
    return np.block(
        [
            [np.kron(eye, c), np.kron(eye, -direction * s)],
            [np.kron(eye, direction * s), np.kron(eye, c)],
        ]
    )


def look_table():
    table = np.zeros((4, 2, 2, SPLIT, 2, 4, 2, SPLIT // LOOKS))
    for g in range(4):
        for c in range(2):
            for rb in range(2):
                for q in range(SPLIT):
                    table[g, c, rb, q, rb, g, c, q // LOOKS] = 1.0 / LOOKS
    return table.reshape(4 * 2 * 2 * SPLIT, 2 * 4 * 2 * SPLIT // LOOKS)


def patch_azimuth_table():
    c, s = base_tables()
    table = np.zeros((4, 4, 2, 16, 4, 2, 64))
    for p in range(4):
        part_c, part_s = c[16 * p : 16 * p + 16], s[16 * p : 16 * p + 16]
        for r in range(4):
            table[p, r, 0, :, r, 0] = part_c
            table[p, r, 1, :, r, 0] = part_s
            table[p, r, 0, :, r, 1] = -part_s
            table[p, r, 1, :, r, 1] = part_c
    return table.reshape(512, 512)


def patch_range_table():
    c, s = base_tables()
    return np.concatenate([c, s], axis=1)


def back_azimuth_table():
    c, s = base_tables()
    c, s = c[:, 16:48], s[:, 16:48]
    table = np.zeros((4, 2, 64, 2, 4, 32))
    for i in range(4):
        table[i, 0, :, 0, i] = c
        table[i, 1, :, 0, i] = -s
        table[i, 0, :, 1, i] = s
        table[i, 1, :, 1, i] = c
    return table.reshape(512, 256)


def back_range_table():
    c, s = base_tables()
    c, s = c[16:48], s[16:48]
    return np.block([[c, -s], [s, c]])


def dot(a, b):
    return jnp.dot(a, b, preferred_element_type=jnp.float32)


def lane_order():
    lane = np.arange(SPLIT)
    return 2 * (lane % (SPLIT // 2)) + lane // (SPLIT // 2)


def spectrum_side(table, axis):
    order = np.concatenate([SPLIT * half + lane_order() for half in range(4)])
    return np.take(table, order, axis=axis)


def cos_sin(angle):
    h = 0.5 * angle
    h2 = h * h
    sin_h = 1.0 / 6227020800.0
    for fact in (-39916800.0, 362880.0, -5040.0, 120.0, -6.0, 1.0):
        sin_h = sin_h * h2 + 1.0 / fact
    sin_h = sin_h * h
    cos_h = 1.0 / 479001600.0
    for fact in (-3628800.0, 40320.0, -720.0, 24.0, -2.0, 1.0):
        cos_h = cos_h * h2 + 1.0 / fact
    return 1.0 - 2.0 * sin_h * sin_h, 2.0 * sin_h * cos_h


def make_weights(g, band_ref, lines_ref, weight_ref, cos_ref, sin_ref):
    shape = (SPLIT, LANES)
    lane = lax.broadcasted_iota(jnp.int32, shape, 1)
    row = lax.broadcasted_iota(jnp.int32, shape, 0)
    half = SPLIT // 2
    k = row + SPLIT * (2 * (lane & (half - 1)) + ((lane & half) // half))
    total = SPLIT * SPLIT
    f = jnp.where(k < total // 2, k, k - total).astype(jnp.float32)
    ratio = f * (2.0 / total)
    band = jnp.where(lane < SPLIT, band_ref[g], band_ref[g + GROUPS]).astype(jnp.float32)
    s = band * (ratio * ratio - 0.5)
    n = jnp.floor(s + 0.5)
    y = s - n
    y2 = y * y
    pi = math.pi
    poly = -(pi**11) / 39916800.0
    for power, fact in ((9, 362880.0), (7, -5040.0), (5, 120.0), (3, -6.0), (1, 1.0)):
        poly = poly * y2 + (pi**power) / fact
    odd = n.astype(jnp.int32) & 1
    lobe = jnp.where(odd == 1, 1.0, -1.0) * (y * poly) * (1.0 / pi)
    cos_s, sin_s = cos_sin(s * (pi / 4.0))
    cos_s, sin_s = 0.5 * cos_s, 0.5 * sin_s
    for tap in range(TAPS):
        m = tap + 1 - SHIFT
        x = m - s
        sign = 1.0 if m % 2 == 0 else -1.0
        safe = jnp.where(x == 0.0, 1.0, x)
        sinc = jnp.where(x == 0.0, 1.0, (sign * lobe) / safe)
        window = 0.5 + math.cos(pi * m / 4.0) * cos_s + math.sin(pi * m / 4.0) * sin_s
        weight_ref[g, tap] = jnp.where(jnp.abs(x) < SHIFT / 2.0, sinc * window, 0.0)
    first = lines_ref[pl.ds(g, SPLIT // 2, stride=STRIP)]
    second = lines_ref[pl.ds(g + GROUPS, SPLIT // 2, stride=STRIP)]
    pieces = [first, pltpu.roll(first, SPLIT, 1), second, pltpu.roll(second, SPLIT, 1)]
    angle = jnp.concatenate(pieces, axis=0).T[:SPLIT]
    cos_ref[g], sin_ref[g] = cos_sin(angle)


def arrived_lines(wide_ref, g, sources, local, low):
    rows = []
    for c in range(2):
        for pair in range(wide_ref.shape[1]):
            one = wide_ref[c, pair, pl.ds(g, sources, stride=STRIP)]
            two = wide_ref[c, pair, pl.ds(g + GROUPS, sources, stride=STRIP)]
            rows.append(jnp.where(low[:sources], one, pltpu.roll(two, SPLIT, 1)))
            if local > 1:
                rows.append(jnp.where(low[:sources], pltpu.roll(one, SPLIT, 1), two))
    return jnp.concatenate(rows, axis=0).astype(jnp.bfloat16)


def scene_kernel(
    band_ref, packed_ref, phase_ref,
    left_ref, right_ref, back_right_ref, back_left_ref, tc_ref, ts_ref, look_ref,
    azimuth_ref, range_ref, back_azimuth_ref, back_range_ref,
    out_ref,
    raw_ref, spread_ref, recv_ref, lines_ref, wide_ref, weight_ref, cos_ref, sin_ref, ext_ref,
    up_ref, down_ref, before_ref, after_ref, focused_ref, high_ref, low_ref,
    own_ref, own_before_ref, own_after_ref, line_ref, grid_ref,
    send_sem, recv_sem, local_sem, edge_send, edge_recv, look_send, look_recv,
    loads,
):
    scene = lax.axis_size("scene")
    me = lax.axis_index("scene")
    dates = raw_ref.shape[1]
    local = raw_ref.shape[3] // SPLIT
    low = lax.broadcasted_iota(jnp.int32, (SPLIT, LANES), 1) < SPLIT
    patches = SPLIT // 2

    barrier = pltpu.get_barrier_semaphore()

    def greet(o, carry):
        pl.semaphore_signal(
            barrier, inc=1, device_id={"scene": lax.rem(me + o, scene)},
            device_id_type=pl.DeviceIdType.MESH,
        )
        return carry

    lax.fori_loop(1, scene, greet, 0)
    for load in loads:
        load.start()
    loads[0].wait()
    height = packed_ref.shape[0]
    piece = height // 8

    def spread(i, carry):
        rows = pl.ds(pl.multiple_of(i * piece, piece), piece)
        spread_ref[rows] = packed_ref[rows].astype(jnp.float32)
        return carry

    lax.fori_loop(0, 8, spread, 0)
    tiles = raw_ref.shape[2] // LANES
    stride = 2 * tiles * dates

    def turn(d):
        def body(tile, carry):
            for c in range(2):
                start = (c * tiles + tile) * dates + d
                lines = spread_ref[pl.ds(start, raw_ref.shape[3], stride=stride)]
                target = pl.ds(pl.multiple_of(tile * LANES, LANES), LANES)
                raw_ref[c, d, target] = lines.T.astype(jnp.bfloat16)
            return carry

        lax.fori_loop(0, tiles, body, 0)

    turn(0)
    pl.semaphore_wait(barrier, scene - 1)

    def strip_copy(d, o):
        peer = lax.rem(me + o, scene)
        start = pl.multiple_of(peer * STRIP, STRIP)
        return pltpu.make_async_remote_copy(
            src_ref=raw_ref.at[:, d, pl.ds(start, STRIP)],
            dst_ref=recv_ref.at[d, me],
            send_sem=send_sem.at[d, o],
            recv_sem=recv_sem.at[d, o],
            device_id={"scene": peer},
            device_id_type=pl.DeviceIdType.MESH,
        )

    def own_copy(d):
        start = pl.multiple_of(me * STRIP, STRIP)
        return pltpu.make_async_copy(
            raw_ref.at[:, d, pl.ds(start, STRIP)], recv_ref.at[d, me], local_sem.at[d]
        )

    held = scene - scene // 3

    for d in range(dates):

        def send(o, carry):
            strip_copy(d, o).start()
            return carry

        if d:
            turn(d)
        lax.fori_loop(1, held if d else scene, send, 0)
        own_copy(d).start()

    for load in loads[1:]:
        load.wait()

    for part in range(SPLIT // 2):
        lines_ref[pl.ds(part * STRIP, STRIP)] = phase_ref[:, part * LANES : (part + 1) * LANES]

    def weigh(g, carry):
        make_weights(g, band_ref, lines_ref, weight_ref, cos_ref, sin_ref)
        return carry

    lax.fori_loop(0, GROUPS, weigh, 0)

    @pl.when(me == 0)
    def _():
        before_ref[...] = jnp.zeros(before_ref.shape, before_ref.dtype)
        own_before_ref[...] = jnp.zeros(own_before_ref.shape, own_before_ref.dtype)

    @pl.when(me == scene - 1)
    def _():
        after_ref[...] = jnp.zeros(after_ref.shape, after_ref.dtype)
        own_after_ref[...] = jnp.zeros(own_after_ref.shape, own_after_ref.dtype)

    line_ref[...] = jnp.zeros(line_ref.shape, jnp.float32)

    def neighbour(source, target, send, recv, step):
        return pltpu.make_async_remote_copy(
            src_ref=source, dst_ref=target, send_sem=send, recv_sem=recv,
            device_id={"scene": me + step}, device_id_type=pl.DeviceIdType.MESH,
        )

    def edge_copies(d):
        return (
            neighbour(up_ref.at[d], before_ref.at[d], edge_send.at[d, 0], edge_recv.at[d, 0], 1),
            neighbour(down_ref.at[d], after_ref.at[d], edge_send.at[d, 1], edge_recv.at[d, 1], -1),
        )

    def look_copies():
        return (
            neighbour(
                own_ref.at[pl.ds(CHUNKS - HALO_CHUNKS, HALO_CHUNKS)], own_before_ref,
                look_send.at[0], look_recv.at[0], 1,
            ),
            neighbour(
                own_ref.at[pl.ds(0, HALO_CHUNKS)], own_after_ref,
                look_send.at[1], look_recv.at[1], -1,
            ),
        )

    def start_pair(copies):
        @pl.when(me < scene - 1)
        def _():
            copies[0].start()

        @pl.when(me > 0)
        def _():
            copies[1].start()

    def wait_pair(copies):
        @pl.when(me > 0)
        def _():
            copies[0].wait_recv()
            copies[1].wait_send()

        @pl.when(me < scene - 1)
        def _():
            copies[1].wait_recv()
            copies[0].wait_send()

    def focus_date(d):
        wait_pair(edge_copies(d))

        def fill(i, carry):
            before = before_ref[d, i].astype(jnp.float32)
            after = after_ref[d, i].astype(jnp.float32)
            before_parts = (before, pltpu.roll(before, SPLIT, 1))
            after_parts = (pltpu.roll(after, SPLIT, 1), after)
            for c in range(2):
                ext_ref[d, c, i] = jnp.where(low, before_parts[c], ext_ref[d, c, i])
                last = i + 3 * SHIFT
                ext_ref[d, c, last] = jnp.where(low, ext_ref[d, c, last], after_parts[c])
            return carry

        lax.fori_loop(0, SHIFT, fill, 0, unroll=2)

        def focus(g, carry):
            re_sum = jnp.zeros((SPLIT, LANES), jnp.float32)
            im_sum = jnp.zeros((SPLIT, LANES), jnp.float32)
            for tap in range(TAPS):
                weight = weight_ref[g, tap]
                re_sum += weight * ext_ref[d, 0, g + tap + 1]
                im_sum += weight * ext_ref[d, 1, g + tap + 1]
            cos_phase, sin_phase = cos_ref[g], sin_ref[g]
            compressed = jnp.concatenate(
                [re_sum * cos_phase - im_sum * sin_phase, im_sum * cos_phase + re_sum * sin_phase],
                axis=1,
            ).astype(jnp.bfloat16)
            first = dot(compressed, back_right_ref[...])
            re, im = first[:, :LANES], first[:, LANES:]
            tc, ts = tc_ref[...], ts_ref[...]
            segment = jnp.concatenate([re * tc - im * ts, im * tc + re * ts], axis=0)
            second = dot(back_left_ref[...], segment.astype(jnp.bfloat16)) * (1.0 / SPLIT)
            second = second.astype(jnp.bfloat16)
            if d == 0:
                focused_ref[g] = second
                return carry
            leading, trailing = second.astype(jnp.float32), focused_ref[g].astype(jnp.float32)
            lr, li = leading[:SPLIT], leading[SPLIT:]
            tr, ti = trailing[:SPLIT], trailing[SPLIT:]
            product = jnp.concatenate([lr * tr + li * ti, li * tr - lr * ti], axis=1)
            high = product.astype(jnp.bfloat16)
            high_ref[g] = high
            low_ref[g] = (product - high.astype(jnp.float32)).astype(jnp.bfloat16)
            return carry

        lax.fori_loop(0, GROUPS, focus, 0, unroll=8)

    for d in range(dates):

        def arrive(o, carry):
            strip_copy(d, o).wait_recv()
            return carry

        lax.fori_loop(1, scene, arrive, 0)
        own_copy(d).wait()

        def widen(source, carry):
            start = pl.multiple_of(source * STRIP, STRIP)
            for c in range(2):
                strip = recv_ref[d, source, c].astype(jnp.float32)
                for pair in range(wide_ref.shape[1]):
                    part = strip[:, pair * LANES : (pair + 1) * LANES]
                    wide_ref[c, pair, pl.ds(start, STRIP), : part.shape[1]] = part
            return carry

        lax.fori_loop(0, scene, widen, 0)

        def forward(i, carry):
            for half in range(2):
                g = i + half * (GROUPS // 2)
                lines = arrived_lines(wide_ref, g, scene, local, low)
                first = dot(left_ref[...], lines)
                re, im = first[:SPLIT], first[SPLIT:]
                tc, ts = tc_ref[...], ts_ref[...]
                segment = jnp.concatenate([re * tc + im * ts, im * tc - re * ts], axis=1)
                second = dot(segment.astype(jnp.bfloat16), right_ref[...]) * (1.0 / SPLIT)
                second = second.astype(jnp.bfloat16).astype(jnp.float32)
                re, im = second[:, :LANES], second[:, LANES:]
                re_turned, im_turned = pltpu.roll(re, SPLIT, 1), pltpu.roll(im, SPLIT, 1)
                other = i + (0 if half else 3 * SHIFT)
                ext_ref[d, 0, g + SHIFT] = re
                ext_ref[d, 1, g + SHIFT] = im
                ext_ref[d, 0, other] = re_turned
                ext_ref[d, 1, other] = im_turned
                if half == 0:
                    down_ref[d, i] = jnp.where(low, re, im_turned).astype(jnp.bfloat16)
                else:
                    up_ref[d, i] = jnp.where(low, re_turned, im).astype(jnp.bfloat16)
            return carry

        lax.fori_loop(0, GROUPS // 2, forward, 0, unroll=8)
        start_pair(edge_copies(d))
        if d == 0:

            def send_rest(o, carry):
                strip_copy(1, o).start()
                return carry

            lax.fori_loop(held, scene, send_rest, 0)
        focus_date(d)

    for big in range(GROUPS // 4):
        high = jnp.concatenate([high_ref[4 * big + j] for j in range(4)], axis=1)
        rest = jnp.concatenate([low_ref[4 * big + j] for j in range(4)], axis=1)
        looked = dot(high, look_ref[...]) + dot(rest, look_ref[...])
        own_ref[big] = looked[:, :LANES].astype(jnp.bfloat16)
        own_ref[HALO_CHUNKS + big] = looked[:, LANES:].astype(jnp.bfloat16)
    start_pair(look_copies())

    def lines_of(first_chunk, count):
        def forward_lines(step, carry):
            rows = []
            for j in range(4):
                chunk = first_chunk + 4 * step + j
                rows.append(
                    jnp.concatenate(
                        [line_ref[chunk, pl.ds(p, patches, stride=2)] for p in range(4)], axis=1
                    )
                )
            lines = jnp.concatenate(rows, axis=0).astype(jnp.bfloat16)
            result = dot(lines, azimuth_ref[...]).astype(jnp.bfloat16).astype(jnp.float32)
            for j in range(4):
                for r in range(4):
                    start = ((first_chunk + 4 * step + j) * 4 + r) * patches
                    grid_ref[pl.ds(pl.multiple_of(start, patches), patches)] = result[
                        j * patches : (j + 1) * patches, r * LANES : (r + 1) * LANES
                    ]
            return carry

        lax.fori_loop(0, count // 4, forward_lines, 0)

    for j in range(CHUNKS):
        line_ref[HALO_CHUNKS + j, pl.ds(1, SPLIT)] = own_ref[j].astype(jnp.float32)
    lines_of(HALO_CHUNKS, CHUNKS)
    wait_pair(look_copies())
    for j in range(HALO_CHUNKS):
        line_ref[j, pl.ds(1, SPLIT)] = own_before_ref[j].astype(jnp.float32)
        line_ref[HALO_CHUNKS + CHUNKS + j, pl.ds(1, SPLIT)] = own_after_ref[j].astype(jnp.float32)
    lines_of(0, HALO_CHUNKS)
    lines_of(HALO_CHUNKS + CHUNKS, HALO_CHUNKS)
    sign = jnp.where(low, 1.0, -1.0)

    def filter_patches(step, carry):
        tiles = []
        for j in range(4):
            tile = grid_ref[pl.ds(4 * step + j, PATCH, stride=patches)]
            swapped = pltpu.roll(tile, PATCH, 1) * sign
            tiles.append(jnp.concatenate([tile, swapped], axis=0).astype(jnp.bfloat16))
        spectra = dot(range_ref[...], jnp.concatenate(tiles, axis=1)) * (1.0 / PATCH)
        kept = []
        for j in range(4):
            spectrum = spectra[:, j * LANES : (j + 1) * LANES]
            power = spectrum * spectrum
            magnitude = jnp.sqrt(power + pltpu.roll(power, PATCH, 1) + EPSILON)
            row_sum = (
                magnitude
                + pltpu.roll(magnitude, 1, 0)
                + pltpu.roll(magnitude, PATCH - 1, 0)
            )
            smooth = (row_sum + pltpu.roll(row_sum, 1, 1) + pltpu.roll(row_sum, LANES - 1, 1)) * (
                1.0 / 9.0
            )
            level = jnp.sum(jnp.sum(magnitude, axis=0, keepdims=True), axis=1, keepdims=True)
            level = level * (1.0 / (PATCH * LANES)) + EPSILON
            kept.append((spectrum * (smooth / level)).astype(jnp.bfloat16))
        back = dot(jnp.concatenate(kept, axis=1), back_azimuth_ref[...]).astype(jnp.bfloat16)
        stacked = jnp.concatenate([back[:, :LANES], back[:, LANES:]], axis=0)
        result = (dot(back_range_ref[...], stacked) * (1.0 / PATCH)).astype(jnp.bfloat16)
        start = pl.multiple_of(step * LANES, LANES)
        out_ref[:, pl.ds(start, LANES)] = result
        return carry

    lax.fori_loop(0, patches // 4, filter_patches, 0, unroll=4)

    for d in range(dates):

        def sent(o, carry):
            strip_copy(d, o).wait_send()
            return carry

        lax.fori_loop(1, scene, sent, 0)


def loading_kernel(band_ref, *refs):
    held, out_ref, kept, load_sem = refs[:TABLES], refs[TABLES], refs[TABLES + 1 : -1], refs[-1]
    loads = [
        pltpu.make_async_copy(source, target, load_sem.at[i])
        for i, (source, target) in enumerate(zip(held, kept[:TABLES]))
    ]
    scene_kernel(band_ref, *kept[:TABLES], out_ref, *kept[TABLES:], loads)


def run_scene(raw, band, phase, left, scene, shape):
    dates, width = shape[1], shape[3]
    looks = SPLIT * SPLIT // LOOKS
    tc, ts = twiddle_tables()
    vmem = pl.BlockSpec(memory_space=pltpu.VMEM)
    plane = (GROUPS, SPLIT, LANES)
    edge = pltpu.VMEM((dates, SHIFT, SPLIT, LANES), jnp.bfloat16)
    looked_edge = pltpu.VMEM((HALO_CHUNKS, SPLIT, LANES), jnp.bfloat16)
    products = pltpu.VMEM((GROUPS, SPLIT, 2 * LANES), jnp.bfloat16)
    dma = pltpu.SemaphoreType.DMA
    tables = (
        raw, phase, bf16(left), bf16(spectrum_side(right_table(1.0), 1)),
        bf16(spectrum_side(right_table(-1.0), 0)), bf16(left_table(-1.0)),
        jnp.asarray(tc), jnp.asarray(ts), bf16(look_table()),
        bf16(patch_azimuth_table()), bf16(patch_range_table()),
        bf16(back_azimuth_table()), bf16(back_range_table()),
    )
    return pl.pallas_call(
        loading_kernel,
        in_specs=[pl.BlockSpec(memory_space=pltpu.SMEM)]
        + [pl.BlockSpec(memory_space=pl.ANY)] * TABLES,
        out_specs=vmem,
        out_shape=jax.ShapeDtypeStruct((2 * STRIP, looks), jnp.bfloat16),
        scratch_shapes=[pltpu.VMEM(table.shape, table.dtype) for table in tables]
        + [
            pltpu.VMEM(shape, jnp.bfloat16),
            pltpu.VMEM(raw.shape, jnp.float32),
            pltpu.VMEM((dates, scene, 2, STRIP, width), jnp.bfloat16),
            pltpu.VMEM((STRIP * SPLIT // 2, LANES), jnp.float32),
            pltpu.VMEM((2, pl.cdiv(width, LANES), scene * STRIP, LANES), jnp.float32),
            pltpu.VMEM((GROUPS, TAPS, SPLIT, LANES), jnp.float32),
            pltpu.VMEM(plane, jnp.float32),
            pltpu.VMEM(plane, jnp.float32),
            pltpu.VMEM((dates, 2, GROUPS + 2 * SHIFT, SPLIT, LANES), jnp.float32),
            edge, edge, edge, edge,
            pltpu.VMEM((GROUPS, 2 * SPLIT, LANES), jnp.bfloat16),
            products, products,
            pltpu.VMEM((CHUNKS, SPLIT, LANES), jnp.bfloat16),
            looked_edge,
            looked_edge,
            pltpu.VMEM((2 * CHUNKS, SPLIT + 8, LANES), jnp.float32),
            pltpu.VMEM((PATCH * SPLIT // 2, LANES), jnp.float32),
            dma((dates, scene)), dma((dates, scene)), dma((dates,)),
            dma((dates, 2)), dma((dates, 2)), dma((2,)), dma((2,)), dma((TABLES,)),
        ],
        compiler_params=pltpu.CompilerParams(
            vmem_limit_bytes=VMEM_LIMIT, collective_id=0, has_side_effects=True
        ),
        name="scene",
    )(band, *tables)


def on_device(raw_echoes, azimuth_phase, band_offset, partners):
    scene = lax.axis_size("scene")
    dates = raw_echoes.shape[2]
    local = raw_echoes.shape[0] // SPLIT
    pairs = partners.size
    assert dates == 2 and raw_echoes.shape[3] == scene * STRIP
    left = left_table(1.0).reshape(2 * SPLIT, 2, scene, local)
    left = left.transpose(0, 1, 3, 2).reshape(2 * SPLIT, 2 * SPLIT)
    lines, bins = raw_echoes.shape[0], raw_echoes.shape[3]
    raw = raw_echoes.reshape(lines, 2, dates, bins // LANES, LANES)
    raw = raw.transpose(0, 1, 3, 2, 4).reshape(-1, LANES)
    phase = azimuth_phase.T
    result = run_scene(
        raw, band_offset, phase, left, scene, (2, dates, bins, lines)
    )
    result = jnp.broadcast_to(result, (pairs,) + result.shape)
    return result.reshape(pairs, 2, STRIP, -1).transpose(0, 3, 1, 2)


def solution(mesh):
    return jax.shard_map(
        on_device,
        mesh=mesh,
        in_specs=(
            P("scene", None, "stack", None),
            P("stack", "scene"),
            P(("stack", "scene")),
            P("stack", None),
        ),
        out_specs=P("stack", None, None, "scene"),
        check_vma=False,
    )
```

profile of v0, /device:TPU:16, one launch (start us, length us, event | category | flops | bytes accessed | tf_op | source)
XLA Modules:
  0.0 55.8 jit_solution(16394388040174971952)
XLA Ops:
  0.0 54.1 %scene.1 = bf16[64,1024]{1,0:T(8,128)(2,1)} custom-call(s32[32]{0:T(128)} %band_ref.1, bf16[4096,128]{1,0:T(8,128)(2,1)} %bitcast.9, f32[32,4096]{1,0:T(8,128)} %bitcast.11, bf16[128,128]{1,0:T(8,128)(2,1)} %constant.22.clone.refs_2_, bf16[256,256]{1,0:T(8,128)(2,1)} %constant.23.clone.refs_3_, bf16[256,256]{1,0:T(8,128)(2,1)} %constant.24.clone.refs_4_, ...), custom_call_target="tpu_custom_call" | custom-call | tf_op jit(solution)/shard_map/scene/pallas_call | solution.py:549
  54.1 1.6 %broadcast_bitcast_fusion = bf16[2,1024,2,32]{1,3,2,0:T(8,128)(2,1)} fusion(bf16[2,32,1024]{2,1,0:T(8,128)(2,1)} %bitcast.10), kind=kLoop, calls=%fused_computation | loop fusion | bytes 393216 | tf_op jit(solution)/shard_map/transpose | solution.py:600
where the time goes:
time: 55.9 us; the launch traced here: 55.8 us
  Pallas kernels  54.1 us (97%)
  local copies, waits for them, and re-layouts  1.63 us (3%)
    pallas_call x1, Pallas kernels, run_scene(): pl.pallas_call(loading_kernel, in_specs=[pl.BlockSpec(memory_space=pltpu....  54.1 us
    transpose x1, local copies, waits for them, and re-layouts, on_device(): return result.reshape(pairs, 2, STRIP, -1).transpose(0, 3, 1, 2)  1.63 us

commit v1 on v0

--- a/solution.py
+++ b/solution.py
@@ -19,8 +19,10 @@
 LANES = 2 * SPLIT
 CHUNKS = STRIP // 4
 HALO_CHUNKS = CHUNKS // 2
+HALF = STRIP // 2
+EARLY = 12
 TABLES = 13
-VMEM_LIMIT = 56 * 1024 * 1024
+VMEM_LIMIT = 40 * 1024 * 1024
 
 
 def base_tables():
@@ -168,12 +170,12 @@
     cos_ref[g], sin_ref[g] = cos_sin(angle)
 
 
-def arrived_lines(wide_ref, g, sources, local, low):
+def arrived_lines(wide_ref, i, sources, local, low):
     rows = []
     for c in range(2):
         for pair in range(wide_ref.shape[1]):
-            one = wide_ref[c, pair, pl.ds(g, sources, stride=STRIP)]
-            two = wide_ref[c, pair, pl.ds(g + GROUPS, sources, stride=STRIP)]
+            one = wide_ref[c, pair, pl.ds(i, sources, stride=HALF)]
+            two = wide_ref[c, pair, pl.ds(i + SHIFT, sources, stride=HALF)]
             rows.append(jnp.where(low[:sources], one, pltpu.roll(two, SPLIT, 1)))
             if local > 1:
                 rows.append(jnp.where(low[:sources], pltpu.roll(one, SPLIT, 1), two))
@@ -186,15 +188,16 @@
     azimuth_ref, range_ref, back_azimuth_ref, back_range_ref,
     out_ref,
     raw_ref, spread_ref, recv_ref, lines_ref, wide_ref, weight_ref, cos_ref, sin_ref, ext_ref,
-    up_ref, down_ref, before_ref, after_ref, focused_ref, high_ref, low_ref,
+    rim_ref, up_ref, down_ref, before_ref, after_ref, focused_ref,
     own_ref, own_before_ref, own_after_ref, line_ref, grid_ref,
     send_sem, recv_sem, local_sem, edge_send, edge_recv, look_send, look_recv,
     loads,
 ):
     scene = lax.axis_size("scene")
     me = lax.axis_index("scene")
-    dates = raw_ref.shape[1]
-    local = raw_ref.shape[3] // SPLIT
+    dates = raw_ref.shape[0]
+    lines_held = raw_ref.shape[5]
+    local = lines_held // SPLIT
     low = lax.broadcasted_iota(jnp.int32, (SPLIT, LANES), 1) < SPLIT
     patches = SPLIT // 2
 
@@ -220,16 +223,21 @@
         return carry
 
     lax.fori_loop(0, 8, spread, 0)
-    tiles = raw_ref.shape[2] // LANES
+    owners = LANES // STRIP
+    tiles = scene // owners
     stride = 2 * tiles * dates
 
     def turn(d):
         def body(tile, carry):
             for c in range(2):
                 start = (c * tiles + tile) * dates + d
-                lines = spread_ref[pl.ds(start, raw_ref.shape[3], stride=stride)]
-                target = pl.ds(pl.multiple_of(tile * LANES, LANES), LANES)
-                raw_ref[c, d, target] = lines.T.astype(jnp.bfloat16)
+                bins = spread_ref[pl.ds(start, lines_held, stride=stride)].T
+                for n in range(owners):
+                    own = bins[n * STRIP : (n + 1) * STRIP]
+                    rim = jnp.concatenate([own[:SHIFT], own[STRIP - SHIFT :]], axis=0)
+                    core = own[SHIFT : STRIP - SHIFT]
+                    raw_ref[d, 0, tile * owners + n, c] = rim.astype(jnp.bfloat16)
+                    raw_ref[d, 1, tile * owners + n, c] = core.astype(jnp.bfloat16)
             return carry
 
         lax.fori_loop(0, tiles, body, 0)
@@ -237,36 +245,48 @@
     turn(0)
     pl.semaphore_wait(barrier, scene - 1)
 
-    def strip_copy(d, o):
+    def far(i):
+        half = (i + 1) // 2
+        return scene // 2 + half * (1 - 2 * lax.rem(i, 2))
+
+    def piece_of(ref, k, owner):
+        return ref.at[0, :, owner] if k == 0 else ref.at[1, k - 1, owner]
+
+    def strip_copy(k, o):
         peer = lax.rem(me + o, scene)
-        start = pl.multiple_of(peer * STRIP, STRIP)
         return pltpu.make_async_remote_copy(
-            src_ref=raw_ref.at[:, d, pl.ds(start, STRIP)],
-            dst_ref=recv_ref.at[d, me],
-            send_sem=send_sem.at[d, o],
-            recv_sem=recv_sem.at[d, o],
+            src_ref=piece_of(raw_ref, k, peer),
+            dst_ref=piece_of(recv_ref, k, me),
+            send_sem=send_sem.at[k, o],
+            recv_sem=recv_sem.at[k, o],
             device_id={"scene": peer},
             device_id_type=pl.DeviceIdType.MESH,
         )
 
-    def own_copy(d):
-        start = pl.multiple_of(me * STRIP, STRIP)
+    def own_copy(k):
         return pltpu.make_async_copy(
-            raw_ref.at[:, d, pl.ds(start, STRIP)], recv_ref.at[d, me], local_sem.at[d]
+            piece_of(raw_ref, k, me), piece_of(recv_ref, k, me), local_sem.at[k]
         )
 
-    held = scene - scene // 3
-
-    for d in range(dates):
-
-        def send(o, carry):
-            strip_copy(d, o).start()
-            return carry
-
-        if d:
-            turn(d)
-        lax.fori_loop(1, held if d else scene, send, 0)
-        own_copy(d).start()
+    def send_all(k):
+        def send(i, carry):
+            strip_copy(k, far(i)).start()
+            return carry
+
+        lax.fori_loop(0, scene - 1, send, 0)
+        own_copy(k).start()
+
+    def arrive_all(k):
+        def arrive(o, carry):
+            strip_copy(k, o).wait_recv()
+            return carry
+
+        lax.fori_loop(1, scene, arrive, 0)
+        own_copy(k).wait()
+
+    send_all(0)
+    for d in range(1, dates):
+        turn(d)
 
     for load in loads[1:]:
         load.wait()
@@ -278,7 +298,9 @@
         make_weights(g, band_ref, lines_ref, weight_ref, cos_ref, sin_ref)
         return carry
 
-    lax.fori_loop(0, GROUPS, weigh, 0)
+    lax.fori_loop(0, EARLY, weigh, 0)
+    send_all(1)
+    lax.fori_loop(EARLY, GROUPS, weigh, 0)
 
     @pl.when(me == 0)
     def _():
@@ -304,15 +326,15 @@
             neighbour(down_ref.at[d], after_ref.at[d], edge_send.at[d, 1], edge_recv.at[d, 1], -1),
         )
 
-    def look_copies():
+    def look_copies(big):
         return (
             neighbour(
-                own_ref.at[pl.ds(CHUNKS - HALO_CHUNKS, HALO_CHUNKS)], own_before_ref,
-                look_send.at[0], look_recv.at[0], 1,
+                own_ref.at[HALO_CHUNKS + big], own_before_ref.at[big],
+                look_send.at[big, 0], look_recv.at[big, 0], 1,
             ),
             neighbour(
-                own_ref.at[pl.ds(0, HALO_CHUNKS)], own_after_ref,
-                look_send.at[1], look_recv.at[1], -1,
+                own_ref.at[big], own_after_ref.at[big],
+                look_send.at[big, 1], look_recv.at[big, 1], -1,
             ),
         )
 
@@ -336,115 +358,114 @@
             copies[1].wait_recv()
             copies[0].wait_send()
 
-    def focus_date(d):
+    def widen(d, part):
+        def body(source, carry):
+            start = pl.multiple_of(source * HALF, HALF)
+            for c in range(2):
+                strip = recv_ref[d, part, source, c].astype(jnp.float32)
+                for pair in range(wide_ref.shape[1]):
+                    kept = strip[:, pair * LANES : (pair + 1) * LANES]
+                    wide_ref[c, pair, pl.ds(start, HALF), : kept.shape[1]] = kept
+            return carry
+
+        lax.fori_loop(0, scene, body, 0)
+
+    def transform(i):
+        lines = arrived_lines(wide_ref, i, scene, local, low)
+        first = dot(left_ref[...], lines)
+        re, im = first[:SPLIT], first[SPLIT:]
+        tc, ts = tc_ref[...], ts_ref[...]
+        segment = jnp.concatenate([re * tc + im * ts, im * tc - re * ts], axis=1)
+        second = dot(segment.astype(jnp.bfloat16), right_ref[...]) * (1.0 / SPLIT)
+        second = second.astype(jnp.bfloat16).astype(jnp.float32)
+        return second[:, :LANES], second[:, LANES:]
+
+    def forward_rim(d):
+        widen(d, 0)
+
+        def body(i, carry):
+            re, im = transform(i)
+            re_turned, im_turned = pltpu.roll(re, SPLIT, 1), pltpu.roll(im, SPLIT, 1)
+            rim_ref[d, 0, i] = re
+            rim_ref[d, 1, i] = im
+            down_ref[d, i] = jnp.where(low, re, im_turned).astype(jnp.bfloat16)
+            up_ref[d, i] = jnp.where(low, re_turned, im).astype(jnp.bfloat16)
+            return carry
+
+        lax.fori_loop(0, SHIFT, body, 0, unroll=8)
+        start_pair(edge_copies(d))
+
+    def forward_core(d):
+        widen(d, 1)
         wait_pair(edge_copies(d))
 
-        def fill(i, carry):
+        def body(i, carry):
             before = before_ref[d, i].astype(jnp.float32)
             after = after_ref[d, i].astype(jnp.float32)
-            before_parts = (before, pltpu.roll(before, SPLIT, 1))
-            after_parts = (pltpu.roll(after, SPLIT, 1), after)
-            for c in range(2):
-                ext_ref[d, c, i] = jnp.where(low, before_parts[c], ext_ref[d, c, i])
-                last = i + 3 * SHIFT
-                ext_ref[d, c, last] = jnp.where(low, ext_ref[d, c, last], after_parts[c])
-            return carry
-
-        lax.fori_loop(0, SHIFT, fill, 0, unroll=2)
-
-        def focus(g, carry):
-            re_sum = jnp.zeros((SPLIT, LANES), jnp.float32)
-            im_sum = jnp.zeros((SPLIT, LANES), jnp.float32)
-            for tap in range(TAPS):
-                weight = weight_ref[g, tap]
-                re_sum += weight * ext_ref[d, 0, g + tap + 1]
-                im_sum += weight * ext_ref[d, 1, g + tap + 1]
-            cos_phase, sin_phase = cos_ref[g], sin_ref[g]
-            compressed = jnp.concatenate(
-                [re_sum * cos_phase - im_sum * sin_phase, im_sum * cos_phase + re_sum * sin_phase],
-                axis=1,
-            ).astype(jnp.bfloat16)
-            first = dot(compressed, back_right_ref[...])
-            re, im = first[:, :LANES], first[:, LANES:]
-            tc, ts = tc_ref[...], ts_ref[...]
-            segment = jnp.concatenate([re * tc - im * ts, im * tc + re * ts], axis=0)
-            second = dot(back_left_ref[...], segment.astype(jnp.bfloat16)) * (1.0 / SPLIT)
-            second = second.astype(jnp.bfloat16)
-            if d == 0:
-                focused_ref[g] = second
-                return carry
-            leading, trailing = second.astype(jnp.float32), focused_ref[g].astype(jnp.float32)
+            befores = (before, pltpu.roll(before, SPLIT, 1))
+            afters = (pltpu.roll(after, SPLIT, 1), after)
+            for c, core in enumerate(transform(i)):
+                turned = pltpu.roll(core, SPLIT, 1)
+                rim = rim_ref[d, c, i]
+                ext_ref[c, i] = jnp.where(low, befores[c], turned)
+                ext_ref[c, SHIFT + i] = jnp.where(low, rim, core)
+                ext_ref[c, 2 * SHIFT + i] = jnp.where(low, core, rim)
+                ext_ref[c, 3 * SHIFT + i] = jnp.where(low, turned, afters[c])
+            return carry
+
+        lax.fori_loop(0, SHIFT, body, 0, unroll=8)
+
+    def focus(g):
+        re_sum = jnp.zeros((SPLIT, LANES), jnp.float32)
+        im_sum = jnp.zeros((SPLIT, LANES), jnp.float32)
+        for tap in range(TAPS):
+            weight = weight_ref[g, tap]
+            re_sum += weight * ext_ref[0, g + tap + 1]
+            im_sum += weight * ext_ref[1, g + tap + 1]
+        cos_phase, sin_phase = cos_ref[g], sin_ref[g]
+        compressed = jnp.concatenate(
+            [re_sum * cos_phase - im_sum * sin_phase, im_sum * cos_phase + re_sum * sin_phase],
+            axis=1,
+        ).astype(jnp.bfloat16)
+        first = dot(compressed, back_right_ref[...])
+        re, im = first[:, :LANES], first[:, LANES:]
+        tc, ts = tc_ref[...], ts_ref[...]
+        segment = jnp.concatenate([re * tc - im * ts, im * tc + re * ts], axis=0)
+        second = dot(back_left_ref[...], segment.astype(jnp.bfloat16)) * (1.0 / SPLIT)
+        return second.astype(jnp.bfloat16)
+
+    def focus_first(g, carry):
+        focused_ref[g] = focus(g)
+        return carry
+
+    def focus_last(big, carry):
+        highs, rests = [], []
+        for j in range(4):
+            g = 4 * big + j
+            leading, trailing = focus(g).astype(jnp.float32), focused_ref[g].astype(jnp.float32)
             lr, li = leading[:SPLIT], leading[SPLIT:]
             tr, ti = trailing[:SPLIT], trailing[SPLIT:]
             product = jnp.concatenate([lr * tr + li * ti, li * tr - lr * ti], axis=1)
             high = product.astype(jnp.bfloat16)
-            high_ref[g] = high
-            low_ref[g] = (product - high.astype(jnp.float32)).astype(jnp.bfloat16)
-            return carry
-
-        lax.fori_loop(0, GROUPS, focus, 0, unroll=8)
-
-    for d in range(dates):
-
-        def arrive(o, carry):
-            strip_copy(d, o).wait_recv()
-            return carry
-
-        lax.fori_loop(1, scene, arrive, 0)
-        own_copy(d).wait()
-
-        def widen(source, carry):
-            start = pl.multiple_of(source * STRIP, STRIP)
-            for c in range(2):
-                strip = recv_ref[d, source, c].astype(jnp.float32)
-                for pair in range(wide_ref.shape[1]):
-                    part = strip[:, pair * LANES : (pair + 1) * LANES]
-                    wide_ref[c, pair, pl.ds(start, STRIP), : part.shape[1]] = part
-            return carry
-
-        lax.fori_loop(0, scene, widen, 0)
-
-        def forward(i, carry):
-            for half in range(2):
-                g = i + half * (GROUPS // 2)
-                lines = arrived_lines(wide_ref, g, scene, local, low)
-                first = dot(left_ref[...], lines)
-                re, im = first[:SPLIT], first[SPLIT:]
-                tc, ts = tc_ref[...], ts_ref[...]
-                segment = jnp.concatenate([re * tc + im * ts, im * tc - re * ts], axis=1)
-                second = dot(segment.astype(jnp.bfloat16), right_ref[...]) * (1.0 / SPLIT)
-                second = second.astype(jnp.bfloat16).astype(jnp.float32)
-                re, im = second[:, :LANES], second[:, LANES:]
-                re_turned, im_turned = pltpu.roll(re, SPLIT, 1), pltpu.roll(im, SPLIT, 1)
-                other = i + (0 if half else 3 * SHIFT)
-                ext_ref[d, 0, g + SHIFT] = re
-                ext_ref[d, 1, g + SHIFT] = im
-                ext_ref[d, 0, other] = re_turned
-                ext_ref[d, 1, other] = im_turned
-                if half == 0:
-                    down_ref[d, i] = jnp.where(low, re, im_turned).astype(jnp.bfloat16)
-                else:
-                    up_ref[d, i] = jnp.where(low, re_turned, im).astype(jnp.bfloat16)
-            return carry
-
-        lax.fori_loop(0, GROUPS // 2, forward, 0, unroll=8)
-        start_pair(edge_copies(d))
-        if d == 0:
-
-            def send_rest(o, carry):
-                strip_copy(1, o).start()
-                return carry
-
-            lax.fori_loop(held, scene, send_rest, 0)
-        focus_date(d)
-
-    for big in range(GROUPS // 4):
-        high = jnp.concatenate([high_ref[4 * big + j] for j in range(4)], axis=1)
-        rest = jnp.concatenate([low_ref[4 * big + j] for j in range(4)], axis=1)
+            highs.append(high)
+            rests.append((product - high.astype(jnp.float32)).astype(jnp.bfloat16))
+        high, rest = jnp.concatenate(highs, axis=1), jnp.concatenate(rests, axis=1)
         looked = dot(high, look_ref[...]) + dot(rest, look_ref[...])
         own_ref[big] = looked[:, :LANES].astype(jnp.bfloat16)
         own_ref[HALO_CHUNKS + big] = looked[:, LANES:].astype(jnp.bfloat16)
-    start_pair(look_copies())
+        start_pair(look_copies(big))
+        return carry
+
+    arrive_all(0)
+    forward_rim(0)
+    send_all(2)
+    arrive_all(1)
+    forward_rim(1)
+    forward_core(0)
+    lax.fori_loop(0, GROUPS, focus_first, 0, unroll=8)
+    arrive_all(2)
+    forward_core(1)
+    lax.fori_loop(0, GROUPS // 4, focus_last, 0, unroll=2)
 
     def lines_of(first_chunk, count):
         def forward_lines(step, carry):
@@ -471,7 +492,8 @@
     for j in range(CHUNKS):
         line_ref[HALO_CHUNKS + j, pl.ds(1, SPLIT)] = own_ref[j].astype(jnp.float32)
     lines_of(HALO_CHUNKS, CHUNKS)
-    wait_pair(look_copies())
+    for big in range(HALO_CHUNKS):
+        wait_pair(look_copies(big))
     for j in range(HALO_CHUNKS):
         line_ref[j, pl.ds(1, SPLIT)] = own_before_ref[j].astype(jnp.float32)
         line_ref[HALO_CHUNKS + CHUNKS + j, pl.ds(1, SPLIT)] = own_after_ref[j].astype(jnp.float32)
@@ -511,10 +533,10 @@
 
     lax.fori_loop(0, patches // 4, filter_patches, 0, unroll=4)
 
-    for d in range(dates):
+    for k in range(dates + 1):
 
         def sent(o, carry):
-            strip_copy(d, o).wait_send()
+            strip_copy(k, o).wait_send()
             return carry
 
         lax.fori_loop(1, scene, sent, 0)
@@ -537,7 +559,6 @@
     plane = (GROUPS, SPLIT, LANES)
     edge = pltpu.VMEM((dates, SHIFT, SPLIT, LANES), jnp.bfloat16)
     looked_edge = pltpu.VMEM((HALO_CHUNKS, SPLIT, LANES), jnp.bfloat16)
-    products = pltpu.VMEM((GROUPS, SPLIT, 2 * LANES), jnp.bfloat16)
     dma = pltpu.SemaphoreType.DMA
     tables = (
         raw, phase, bf16(left), bf16(spectrum_side(right_table(1.0), 1)),
@@ -551,34 +572,35 @@
         in_specs=[pl.BlockSpec(memory_space=pltpu.SMEM)]
         + [pl.BlockSpec(memory_space=pl.ANY)] * TABLES,
         out_specs=vmem,
-        out_shape=jax.ShapeDtypeStruct((2 * STRIP, looks), jnp.bfloat16),
+        out_shape=pltpu.VMEM((2 * STRIP, looks), jnp.bfloat16),
         scratch_shapes=[pltpu.VMEM(table.shape, table.dtype) for table in tables]
         + [
-            pltpu.VMEM(shape, jnp.bfloat16),
+            pltpu.VMEM((dates, 2, scene, 2, HALF, width), jnp.bfloat16),
             pltpu.VMEM(raw.shape, jnp.float32),
-            pltpu.VMEM((dates, scene, 2, STRIP, width), jnp.bfloat16),
+            pltpu.VMEM((dates, 2, scene, 2, HALF, width), jnp.bfloat16),
             pltpu.VMEM((STRIP * SPLIT // 2, LANES), jnp.float32),
-            pltpu.VMEM((2, pl.cdiv(width, LANES), scene * STRIP, LANES), jnp.float32),
+            pltpu.VMEM((2, pl.cdiv(width, LANES), scene * HALF, LANES), jnp.float32),
             pltpu.VMEM((GROUPS, TAPS, SPLIT, LANES), jnp.float32),
             pltpu.VMEM(plane, jnp.float32),
             pltpu.VMEM(plane, jnp.float32),
-            pltpu.VMEM((dates, 2, GROUPS + 2 * SHIFT, SPLIT, LANES), jnp.float32),
+            pltpu.VMEM((2, GROUPS + 2 * SHIFT, SPLIT, LANES), jnp.float32),
+            pltpu.VMEM((dates, 2, SHIFT, SPLIT, LANES), jnp.float32),
             edge, edge, edge, edge,
             pltpu.VMEM((GROUPS, 2 * SPLIT, LANES), jnp.bfloat16),
-            products, products,
             pltpu.VMEM((CHUNKS, SPLIT, LANES), jnp.bfloat16),
             looked_edge,
             looked_edge,
             pltpu.VMEM((2 * CHUNKS, SPLIT + 8, LANES), jnp.float32),
             pltpu.VMEM((PATCH * SPLIT // 2, LANES), jnp.float32),
-            dma((dates, scene)), dma((dates, scene)), dma((dates,)),
-            dma((dates, 2)), dma((dates, 2)), dma((2,)), dma((2,)), dma((TABLES,)),
+            dma((dates + 1, scene)), dma((dates + 1, scene)), dma((dates + 1,)),
+            dma((dates, 2)), dma((dates, 2)),
+            dma((HALO_CHUNKS, 2)), dma((HALO_CHUNKS, 2)), dma((TABLES,)),
         ],
         compiler_params=pltpu.CompilerParams(
             vmem_limit_bytes=VMEM_LIMIT, collective_id=0, has_side_effects=True
         ),
         name="scene",
-    )(band, *tables)
+    )(*[pltpu.with_memory_space_constraint(t, pltpu.HBM) for t in (band, *tables)])
 
 
 def on_device(raw_echoes, azimuth_phase, band_offset, partners):

time: 55.9 us -> 48.7 us (0.87)
  the two profiles are of different devices: /device:TPU:16 before, /device:TPU:1 now
where the time goes in v1:
time: 48.7 us; the launch traced here: 47.8 us
  Pallas kernels  47.1 us (97%)
  local copies, waits for them, and re-layouts  0.73 us (1%)
    pallas_call x1, Pallas kernels, run_scene(): pl.pallas_call(loading_kernel, in_specs=[pl.BlockSpec(memory_space=pltpu....  47.1 us

profile of v1, /device:TPU:1, one launch (start us, length us, event | category | flops | bytes accessed | tf_op | source)
XLA Modules:
  0.0 47.8 jit_solution(13605544175934698618)
XLA Ops:
  0.0 47.1 %scene.1 = bf16[64,1024]{1,0:T(8,128)(2,1)S(1)} custom-call(s32[32]{0:T(128)} %band_ref.1, bf16[4096,128]{1,0:T(8,128)(2,1)} %bitcast.10, f32[32,4096]{1,0:T(8,128)} %bitcast.11, bf16[128,128]{1,0:T(8,128)(2,1)} %constant.22.clone.refs_2_, bf16[256,256]{1,0:T(8,128)(2,1)} %constant.23.clone.refs_3_, bf16[256,256]{1,0:T(8,128)(2,1)} %constant.24.clone.refs_4_, ...), custom_call_target="tpu_custom_call" | custom-call | tf_op jit(solution)/shard_map/scene/pallas_call | solution.py:570
  47.1 0.7 %broadcast_bitcast_fusion = bf16[2,1024,2,32]{1,3,2,0:T(8,128)(2,1)} fusion(bf16[2,32,1024]{2,1,0:T(8,128)(2,1)S(1)} %bitcast.9), kind=kLoop, calls=%fused_computation | loop fusion | bytes 393216 | tf_op jit(solution)/shard_map/transpose | solution.py:622

commit v2 on v1

--- a/solution.py
+++ b/solution.py
@@ -20,7 +20,8 @@
 CHUNKS = STRIP // 4
 HALO_CHUNKS = CHUNKS // 2
 HALF = STRIP // 2
-EARLY = 12
+BATCH = 8
+STEPS = 4
 TABLES = 13
 VMEM_LIMIT = 40 * 1024 * 1024
 
@@ -85,18 +86,18 @@
 
 def patch_range_table():
     c, s = base_tables()
-    return np.concatenate([c, s], axis=1)
+    return np.block([[c, s], [-s, c]])
 
 
 def back_azimuth_table():
     c, s = base_tables()
     c, s = c[:, 16:48], s[:, 16:48]
-    table = np.zeros((4, 2, 64, 2, 4, 32))
+    table = np.zeros((2, 4, 64, 2, 4, 32))
     for i in range(4):
-        table[i, 0, :, 0, i] = c
-        table[i, 1, :, 0, i] = -s
-        table[i, 0, :, 1, i] = s
-        table[i, 1, :, 1, i] = c
+        table[0, i, :, 0, i] = c
+        table[1, i, :, 0, i] = -s
+        table[0, i, :, 1, i] = s
+        table[1, i, :, 1, i] = c
     return table.reshape(512, 256)
 
 
@@ -162,7 +163,8 @@
         safe = jnp.where(x == 0.0, 1.0, x)
         sinc = jnp.where(x == 0.0, 1.0, (sign * lobe) / safe)
         window = 0.5 + math.cos(pi * m / 4.0) * cos_s + math.sin(pi * m / 4.0) * sin_s
-        weight_ref[g, tap] = jnp.where(jnp.abs(x) < SHIFT / 2.0, sinc * window, 0.0)
+        weight = jnp.where(jnp.abs(x) < SHIFT / 2.0, sinc * window, 0.0)
+        weight_ref[g, tap] = jnp.concatenate([weight, weight], axis=1).astype(jnp.bfloat16)
     first = lines_ref[pl.ds(g, SPLIT // 2, stride=STRIP)]
     second = lines_ref[pl.ds(g + GROUPS, SPLIT // 2, stride=STRIP)]
     pieces = [first, pltpu.roll(first, SPLIT, 1), second, pltpu.roll(second, SPLIT, 1)]
@@ -199,6 +201,7 @@
     lines_held = raw_ref.shape[5]
     local = lines_held // SPLIT
     low = lax.broadcasted_iota(jnp.int32, (SPLIT, LANES), 1) < SPLIT
+    lows = jnp.concatenate([low, low], axis=1)
     patches = SPLIT // 2
 
     barrier = pltpu.get_barrier_semaphore()
@@ -250,7 +253,7 @@
         return scene // 2 + half * (1 - 2 * lax.rem(i, 2))
 
     def piece_of(ref, k, owner):
-        return ref.at[0, :, owner] if k == 0 else ref.at[1, k - 1, owner]
+        return ref.at[k // 2, k % 2, owner]
 
     def strip_copy(k, o):
         peer = lax.rem(me + o, scene)
@@ -287,6 +290,7 @@
     send_all(0)
     for d in range(1, dates):
         turn(d)
+        send_all(2 * d)
 
     for load in loads[1:]:
         load.wait()
@@ -298,9 +302,7 @@
         make_weights(g, band_ref, lines_ref, weight_ref, cos_ref, sin_ref)
         return carry
 
-    lax.fori_loop(0, EARLY, weigh, 0)
-    send_all(1)
-    lax.fori_loop(EARLY, GROUPS, weigh, 0)
+    lax.fori_loop(0, GROUPS, weigh, 0)
 
     @pl.when(me == 0)
     def _():
@@ -322,8 +324,14 @@
 
     def edge_copies(d):
         return (
-            neighbour(up_ref.at[d], before_ref.at[d], edge_send.at[d, 0], edge_recv.at[d, 0], 1),
-            neighbour(down_ref.at[d], after_ref.at[d], edge_send.at[d, 1], edge_recv.at[d, 1], -1),
+            neighbour(
+                up_ref.at[d, pl.ds(1, SHIFT - 1)], before_ref.at[d, pl.ds(1, SHIFT - 1)],
+                edge_send.at[d, 0], edge_recv.at[d, 0], 1,
+            ),
+            neighbour(
+                down_ref.at[d, pl.ds(0, SHIFT - 1)], after_ref.at[d, pl.ds(0, SHIFT - 1)],
+                edge_send.at[d, 1], edge_recv.at[d, 1], -1,
+            ),
         )
 
     def look_copies(big):
@@ -370,102 +378,129 @@
 
         lax.fori_loop(0, scene, body, 0)
 
-    def transform(i):
-        lines = arrived_lines(wide_ref, i, scene, local, low)
-        first = dot(left_ref[...], lines)
-        re, im = first[:SPLIT], first[SPLIT:]
+    def transform(first, count):
+        held = [arrived_lines(wide_ref, first + n, scene, local, low) for n in range(count)]
+        mixed = dot(left_ref[...], jnp.concatenate(held, axis=1))
         tc, ts = tc_ref[...], ts_ref[...]
-        segment = jnp.concatenate([re * tc + im * ts, im * tc - re * ts], axis=1)
-        second = dot(segment.astype(jnp.bfloat16), right_ref[...]) * (1.0 / SPLIT)
-        second = second.astype(jnp.bfloat16).astype(jnp.float32)
-        return second[:, :LANES], second[:, LANES:]
+        segments = []
+        for n in range(count):
+            re, im = (mixed[k : k + SPLIT, n * LANES : (n + 1) * LANES] for k in (0, SPLIT))
+            segments.append(jnp.concatenate([re * tc + im * ts, im * tc - re * ts], axis=1))
+        stacked = jnp.concatenate(segments, axis=0).astype(jnp.bfloat16)
+        spectra = dot(stacked, right_ref[...]) * (1.0 / SPLIT)
+        return [spectra[n * SPLIT : (n + 1) * SPLIT] for n in range(count)]
+
+    def turned(pair):
+        parts = (pair[:, :LANES], pair[:, LANES:])
+        return jnp.concatenate([pltpu.roll(part, SPLIT, 1) for part in parts], axis=1)
 
     def forward_rim(d):
         widen(d, 0)
 
-        def body(i, carry):
-            re, im = transform(i)
-            re_turned, im_turned = pltpu.roll(re, SPLIT, 1), pltpu.roll(im, SPLIT, 1)
-            rim_ref[d, 0, i] = re
-            rim_ref[d, 1, i] = im
-            down_ref[d, i] = jnp.where(low, re, im_turned).astype(jnp.bfloat16)
-            up_ref[d, i] = jnp.where(low, re_turned, im).astype(jnp.bfloat16)
-            return carry
-
-        lax.fori_loop(0, SHIFT, body, 0, unroll=8)
+        def body(step, carry):
+            for n, rim in enumerate(transform(BATCH * step, BATCH)):
+                i = BATCH * step + n
+                flipped = turned(rim)
+                rim_ref[d, i] = rim
+                down = jnp.where(low, rim[:, :LANES], flipped[:, LANES:])
+                up = jnp.where(low, flipped[:, :LANES], rim[:, LANES:])
+                down_ref[d, i] = down.astype(jnp.bfloat16)
+                up_ref[d, i] = up.astype(jnp.bfloat16)
+            return carry
+
+        lax.fori_loop(0, SHIFT // BATCH, body, 0, unroll=True)
         start_pair(edge_copies(d))
 
     def forward_core(d):
         widen(d, 1)
         wait_pair(edge_copies(d))
 
-        def body(i, carry):
-            before = before_ref[d, i].astype(jnp.float32)
-            after = after_ref[d, i].astype(jnp.float32)
-            befores = (before, pltpu.roll(before, SPLIT, 1))
-            afters = (pltpu.roll(after, SPLIT, 1), after)
-            for c, core in enumerate(transform(i)):
-                turned = pltpu.roll(core, SPLIT, 1)
-                rim = rim_ref[d, c, i]
-                ext_ref[c, i] = jnp.where(low, befores[c], turned)
-                ext_ref[c, SHIFT + i] = jnp.where(low, rim, core)
-                ext_ref[c, 2 * SHIFT + i] = jnp.where(low, core, rim)
-                ext_ref[c, 3 * SHIFT + i] = jnp.where(low, turned, afters[c])
-            return carry
-
-        lax.fori_loop(0, SHIFT, body, 0, unroll=8)
-
-    def focus(g):
-        re_sum = jnp.zeros((SPLIT, LANES), jnp.float32)
-        im_sum = jnp.zeros((SPLIT, LANES), jnp.float32)
-        for tap in range(TAPS):
-            weight = weight_ref[g, tap]
-            re_sum += weight * ext_ref[0, g + tap + 1]
-            im_sum += weight * ext_ref[1, g + tap + 1]
-        cos_phase, sin_phase = cos_ref[g], sin_ref[g]
-        compressed = jnp.concatenate(
-            [re_sum * cos_phase - im_sum * sin_phase, im_sum * cos_phase + re_sum * sin_phase],
-            axis=1,
-        ).astype(jnp.bfloat16)
-        first = dot(compressed, back_right_ref[...])
-        re, im = first[:, :LANES], first[:, LANES:]
+        def body(step, carry):
+            for n, core in enumerate(transform(BATCH * step, BATCH)):
+                i = BATCH * step + n
+                before = before_ref[d, i].astype(jnp.float32)
+                after = after_ref[d, i].astype(jnp.float32)
+                before = jnp.concatenate([before, pltpu.roll(before, SPLIT, 1)], axis=1)
+                after = jnp.concatenate([pltpu.roll(after, SPLIT, 1), after], axis=1)
+                rim, flipped = rim_ref[d, i], turned(core)
+                ext_ref[i] = jnp.where(lows, before, flipped).astype(jnp.bfloat16)
+                ext_ref[SHIFT + i] = jnp.where(lows, rim, core).astype(jnp.bfloat16)
+                ext_ref[2 * SHIFT + i] = jnp.where(lows, core, rim).astype(jnp.bfloat16)
+                ext_ref[3 * SHIFT + i] = jnp.where(lows, flipped, after).astype(jnp.bfloat16)
+            return carry
+
+        lax.fori_loop(0, SHIFT // BATCH, body, 0, unroll=True)
+
+    def migrate(big):
+        totals = [[] for _ in range(4)]
+        for top in range(0, SPLIT, 8):
+            rows = slice(top, top + 8)
+            data = [ext_ref[4 * big + n + 1, rows] for n in range(TAPS + 3)]
+            for j in range(4):
+                sums = []
+                for first in range(2):
+                    total = weight_ref[4 * big + j, first, rows] * data[j + first]
+                    for tap in range(first + 2, TAPS, 2):
+                        total += weight_ref[4 * big + j, tap, rows] * data[j + tap]
+                    sums.append(total.astype(jnp.float32))
+                totals[j].append(sums[0] + sums[1])
+        return [jnp.concatenate(total, axis=0) for total in totals]
+
+    def focus(big):
+        compressed = []
+        for j, migrated in enumerate(migrate(big)):
+            re, im = migrated[:, :LANES], migrated[:, LANES:]
+            cos_phase, sin_phase = cos_ref[4 * big + j], sin_ref[4 * big + j]
+            parts = [re * cos_phase - im * sin_phase, im * cos_phase + re * sin_phase]
+            compressed.append(jnp.concatenate(parts, axis=1).astype(jnp.bfloat16))
+        first = dot(jnp.concatenate(compressed, axis=0), back_right_ref[...])
         tc, ts = tc_ref[...], ts_ref[...]
-        segment = jnp.concatenate([re * tc - im * ts, im * tc + re * ts], axis=0)
-        second = dot(back_left_ref[...], segment.astype(jnp.bfloat16)) * (1.0 / SPLIT)
-        return second.astype(jnp.bfloat16)
-
-    def focus_first(g, carry):
-        focused_ref[g] = focus(g)
+        segments = []
+        for j in range(4):
+            rows = first[j * SPLIT : (j + 1) * SPLIT]
+            re, im = rows[:, :LANES], rows[:, LANES:]
+            segments.append(jnp.concatenate([re * tc - im * ts, im * tc + re * ts], axis=0))
+        stacked = jnp.concatenate(segments, axis=1).astype(jnp.bfloat16)
+        second = (dot(back_left_ref[...], stacked) * (1.0 / SPLIT)).astype(jnp.bfloat16)
+        return [second[:, j * LANES : (j + 1) * LANES] for j in range(4)]
+
+    def focus_first(big, carry):
+        for j, focused in enumerate(focus(big)):
+            focused_ref[4 * big + j] = focused
         return carry
 
-    def focus_last(big, carry):
-        highs, rests = [], []
-        for j in range(4):
-            g = 4 * big + j
-            leading, trailing = focus(g).astype(jnp.float32), focused_ref[g].astype(jnp.float32)
-            lr, li = leading[:SPLIT], leading[SPLIT:]
-            tr, ti = trailing[:SPLIT], trailing[SPLIT:]
-            product = jnp.concatenate([lr * tr + li * ti, li * tr - lr * ti], axis=1)
-            high = product.astype(jnp.bfloat16)
-            highs.append(high)
-            rests.append((product - high.astype(jnp.float32)).astype(jnp.bfloat16))
-        high, rest = jnp.concatenate(highs, axis=1), jnp.concatenate(rests, axis=1)
-        looked = dot(high, look_ref[...]) + dot(rest, look_ref[...])
-        own_ref[big] = looked[:, :LANES].astype(jnp.bfloat16)
-        own_ref[HALO_CHUNKS + big] = looked[:, LANES:].astype(jnp.bfloat16)
-        start_pair(look_copies(big))
+    def focus_last(step, carry):
+        products = []
+        for n in range(2):
+            big = 2 * step + n
+            pieces = []
+            for j, focused in enumerate(focus(big)):
+                leading = focused.astype(jnp.float32)
+                trailing = focused_ref[4 * big + j].astype(jnp.float32)
+                lr, li = leading[:SPLIT], leading[SPLIT:]
+                tr, ti = trailing[:SPLIT], trailing[SPLIT:]
+                product = jnp.concatenate([lr * tr + li * ti, li * tr - lr * ti], axis=1)
+                pieces.append(product.astype(jnp.bfloat16))
+            products.append(jnp.concatenate(pieces, axis=1))
+        looked = dot(jnp.concatenate(products, axis=0), look_ref[...]).astype(jnp.bfloat16)
+        for n in range(2):
+            big, rows = 2 * step + n, slice(n * SPLIT, (n + 1) * SPLIT)
+            own_ref[big] = looked[rows, :LANES]
+            own_ref[HALO_CHUNKS + big] = looked[rows, LANES:]
+            start_pair(look_copies(big))
         return carry
 
-    arrive_all(0)
-    forward_rim(0)
-    send_all(2)
+    send_all(1)
+    for d in range(dates):
+        arrive_all(2 * d)
+        forward_rim(d)
+    send_all(3)
     arrive_all(1)
-    forward_rim(1)
     forward_core(0)
-    lax.fori_loop(0, GROUPS, focus_first, 0, unroll=8)
-    arrive_all(2)
+    lax.fori_loop(0, GROUPS // 4, focus_first, 0, unroll=2)
+    arrive_all(3)
     forward_core(1)
-    lax.fori_loop(0, GROUPS // 4, focus_last, 0, unroll=2)
+    lax.fori_loop(0, GROUPS // 8, focus_last, 0)
 
     def lines_of(first_chunk, count):
         def forward_lines(step, carry):
@@ -492,6 +527,14 @@
     for j in range(CHUNKS):
         line_ref[HALO_CHUNKS + j, pl.ds(1, SPLIT)] = own_ref[j].astype(jnp.float32)
     lines_of(HALO_CHUNKS, CHUNKS)
+    for k in range(2 * dates):
+
+        def sent(o, carry):
+            strip_copy(k, o).wait_send()
+            return carry
+
+        lax.fori_loop(1, scene, sent, 0)
+
     for big in range(HALO_CHUNKS):
         wait_pair(look_copies(big))
     for j in range(HALO_CHUNKS):
@@ -499,47 +542,49 @@
         line_ref[HALO_CHUNKS + CHUNKS + j, pl.ds(1, SPLIT)] = own_after_ref[j].astype(jnp.float32)
     lines_of(0, HALO_CHUNKS)
     lines_of(HALO_CHUNKS + CHUNKS, HALO_CHUNKS)
-    sign = jnp.where(low, 1.0, -1.0)
+    lane = lax.broadcasted_iota(jnp.int32, (PATCH, LANES), 1)
+    opening, closing = lane % PATCH == 0, lane % PATCH == PATCH - 1
 
     def filter_patches(step, carry):
-        tiles = []
-        for j in range(4):
-            tile = grid_ref[pl.ds(4 * step + j, PATCH, stride=patches)]
-            swapped = pltpu.roll(tile, PATCH, 1) * sign
-            tiles.append(jnp.concatenate([tile, swapped], axis=0).astype(jnp.bfloat16))
-        spectra = dot(range_ref[...], jnp.concatenate(tiles, axis=1)) * (1.0 / PATCH)
-        kept = []
-        for j in range(4):
-            spectrum = spectra[:, j * LANES : (j + 1) * LANES]
-            power = spectrum * spectrum
-            magnitude = jnp.sqrt(power + pltpu.roll(power, PATCH, 1) + EPSILON)
-            row_sum = (
-                magnitude
-                + pltpu.roll(magnitude, 1, 0)
-                + pltpu.roll(magnitude, PATCH - 1, 0)
-            )
-            smooth = (row_sum + pltpu.roll(row_sum, 1, 1) + pltpu.roll(row_sum, LANES - 1, 1)) * (
-                1.0 / 9.0
-            )
-            level = jnp.sum(jnp.sum(magnitude, axis=0, keepdims=True), axis=1, keepdims=True)
-            level = level * (1.0 / (PATCH * LANES)) + EPSILON
-            kept.append((spectrum * (smooth / level)).astype(jnp.bfloat16))
-        back = dot(jnp.concatenate(kept, axis=1), back_azimuth_ref[...]).astype(jnp.bfloat16)
-        stacked = jnp.concatenate([back[:, :LANES], back[:, LANES:]], axis=0)
-        result = (dot(back_range_ref[...], stacked) * (1.0 / PATCH)).astype(jnp.bfloat16)
-        start = pl.multiple_of(step * LANES, LANES)
-        out_ref[:, pl.ds(start, LANES)] = result
+        stacks = []
+        for pair in range(2 * STEPS):
+            one = grid_ref[pl.ds(4 * STEPS * step + 2 * pair, PATCH, stride=patches)]
+            two = grid_ref[pl.ds(4 * STEPS * step + 2 * pair + 1, PATCH, stride=patches)]
+            re = jnp.where(low, one, pltpu.roll(two, PATCH, 1))
+            im = jnp.where(low, pltpu.roll(one, PATCH, 1), two)
+            stacks.append(jnp.concatenate([re, im], axis=0).astype(jnp.bfloat16))
+        spectra = dot(range_ref[...], jnp.concatenate(stacks, axis=1)) * (1.0 / PATCH)
+        kept_re, kept_im = [], []
+        for pair in range(2 * STEPS):
+            re = spectra[:PATCH, pair * LANES : (pair + 1) * LANES]
+            im = spectra[PATCH:, pair * LANES : (pair + 1) * LANES]
+            magnitude = jnp.sqrt(re * re + im * im + EPSILON)
+            rows = magnitude + pltpu.roll(magnitude, 1, 0) + pltpu.roll(magnitude, PATCH - 1, 0)
+            left = jnp.where(opening, pltpu.roll(rows, PATCH + 1, 1), pltpu.roll(rows, 1, 1))
+            right = jnp.where(closing, pltpu.roll(rows, PATCH - 1, 1), pltpu.roll(rows, LANES - 1, 1))
+            column = jnp.sum(magnitude, axis=0, keepdims=True)
+            first = jnp.sum(jnp.where(low[:1], column, 0.0), axis=1, keepdims=True)
+            second = jnp.sum(jnp.where(low[:1], 0.0, column), axis=1, keepdims=True)
+            level = jnp.where(low[:1], first, second) * (1.0 / (PATCH * PATCH)) + EPSILON
+            gain = (rows + left + right) * ((1.0 / 9.0) / level)
+            kept_re.append((re * gain).astype(jnp.bfloat16))
+            kept_im.append((im * gain).astype(jnp.bfloat16))
+        kept = [
+            jnp.concatenate(kept_re[2 * n : 2 * n + 2] + kept_im[2 * n : 2 * n + 2], axis=1)
+            for n in range(STEPS)
+        ]
+        back = dot(jnp.concatenate(kept, axis=0), back_azimuth_ref[...]).astype(jnp.bfloat16)
+        stacked = []
+        for n in range(STEPS):
+            rows = back[n * PATCH : (n + 1) * PATCH]
+            stacked.append(jnp.concatenate([rows[:, :LANES], rows[:, LANES:]], axis=0))
+        result = dot(back_range_ref[...], jnp.concatenate(stacked, axis=1)) * (1.0 / PATCH)
+        width = STEPS * LANES
+        start = pl.multiple_of(step * width, width)
+        out_ref[:, pl.ds(start, width)] = result.astype(jnp.bfloat16)
         return carry
 
-    lax.fori_loop(0, patches // 4, filter_patches, 0, unroll=4)
-
-    for k in range(dates + 1):
-
-        def sent(o, carry):
-            strip_copy(k, o).wait_send()
-            return carry
-
-        lax.fori_loop(1, scene, sent, 0)
+    lax.fori_loop(0, patches // (4 * STEPS), filter_patches, 0)
 
 
 def loading_kernel(band_ref, *refs):
@@ -580,11 +625,11 @@
             pltpu.VMEM((dates, 2, scene, 2, HALF, width), jnp.bfloat16),
             pltpu.VMEM((STRIP * SPLIT // 2, LANES), jnp.float32),
             pltpu.VMEM((2, pl.cdiv(width, LANES), scene * HALF, LANES), jnp.float32),
-            pltpu.VMEM((GROUPS, TAPS, SPLIT, LANES), jnp.float32),
+            pltpu.VMEM((GROUPS, TAPS, SPLIT, 2 * LANES), jnp.bfloat16),
             pltpu.VMEM(plane, jnp.float32),
             pltpu.VMEM(plane, jnp.float32),
-            pltpu.VMEM((2, GROUPS + 2 * SHIFT, SPLIT, LANES), jnp.float32),
-            pltpu.VMEM((dates, 2, SHIFT, SPLIT, LANES), jnp.float32),
+            pltpu.VMEM((GROUPS + 2 * SHIFT, SPLIT, 2 * LANES), jnp.bfloat16),
+            pltpu.VMEM((dates, SHIFT, SPLIT, 2 * LANES), jnp.float32),
             edge, edge, edge, edge,
             pltpu.VMEM((GROUPS, 2 * SPLIT, LANES), jnp.bfloat16),
             pltpu.VMEM((CHUNKS, SPLIT, LANES), jnp.bfloat16),
@@ -592,7 +637,7 @@
             looked_edge,
             pltpu.VMEM((2 * CHUNKS, SPLIT + 8, LANES), jnp.float32),
             pltpu.VMEM((PATCH * SPLIT // 2, LANES), jnp.float32),
-            dma((dates + 1, scene)), dma((dates + 1, scene)), dma((dates + 1,)),
+            dma((2 * dates, scene)), dma((2 * dates, scene)), dma((2 * dates,)),
             dma((dates, 2)), dma((dates, 2)),
             dma((HALO_CHUNKS, 2)), dma((HALO_CHUNKS, 2)), dma((TABLES,)),
         ],

time: 48.7 us -> 43 us (0.88); the launches traced: 47.8 us -> 42.9 us
  Pallas kernels: 47.1 us -> 42.1 us
    pallas_call x1, Pallas kernels: 47.1 us -> 42.1 us  [run_scene(): pl.pallas_call(loading_kernel, in_specs=[pl.BlockSpec(memory_space=pltpu....]
where the time goes in v2:
time: 43 us; the launch traced here: 42.9 us
  Pallas kernels  42.1 us (98%)
  local copies, waits for them, and re-layouts  0.73 us (2%)
    pallas_call x1, Pallas kernels, run_scene(): pl.pallas_call(loading_kernel, in_specs=[pl.BlockSpec(memory_space=pltpu....  42.1 us

profile of v2, /device:TPU:1, one launch (start us, length us, event | category | flops | bytes accessed | tf_op | source)
XLA Modules:
  0.0 42.9 jit_solution(13672521339067411507)
XLA Ops:
  0.0 42.1 %scene.1 = bf16[64,1024]{1,0:T(8,128)(2,1)S(1)} custom-call(s32[32]{0:T(128)} %band_ref.1, bf16[4096,128]{1,0:T(8,128)(2,1)} %bitcast.10, f32[32,4096]{1,0:T(8,128)} %bitcast.11, bf16[128,128]{1,0:T(8,128)(2,1)} %constant.22.clone.refs_2_, bf16[256,256]{1,0:T(8,128)(2,1)} %constant.23.clone.refs_3_, bf16[256,256]{1,0:T(8,128)(2,1)} %constant.24.clone.refs_4_, ...), custom_call_target="tpu_custom_call" | custom-call | tf_op jit(solution)/shard_map/scene/pallas_call | solution.py:615
  42.1 0.7 %broadcast_bitcast_fusion = bf16[2,1024,2,32]{1,3,2,0:T(8,128)(2,1)} fusion(bf16[2,32,1024]{2,1,0:T(8,128)(2,1)S(1)} %bitcast.9), kind=kLoop, calls=%fused_computation | loop fusion | bytes 393216 | tf_op jit(solution)/shard_map/transpose | solution.py:667

commit v3 on v2

--- a/solution.py
+++ b/solution.py
@@ -22,7 +22,8 @@
 HALF = STRIP // 2
 BATCH = 8
 STEPS = 4
-TABLES = 13
+TABLES = 5
+SLABS = 4
 VMEM_LIMIT = 40 * 1024 * 1024
 
 
@@ -185,15 +186,13 @@
 
 
 def scene_kernel(
-    band_ref, packed_ref, phase_ref,
-    left_ref, right_ref, back_right_ref, back_left_ref, tc_ref, ts_ref, look_ref,
-    azimuth_ref, range_ref, back_azimuth_ref, back_range_ref,
+    packed_ref, band_ref, phase_ref, table_ref, twiddle_ref,
     out_ref,
     raw_ref, spread_ref, recv_ref, lines_ref, wide_ref, weight_ref, cos_ref, sin_ref, ext_ref,
     rim_ref, up_ref, down_ref, before_ref, after_ref, focused_ref,
     own_ref, own_before_ref, own_after_ref, line_ref, grid_ref,
-    send_sem, recv_sem, local_sem, edge_send, edge_recv, look_send, look_recv,
-    loads,
+    send_sem, recv_sem, edge_send, edge_recv, look_send, look_recv,
+    slabs, loads,
 ):
     scene = lax.axis_size("scene")
     me = lax.axis_index("scene")
@@ -204,6 +203,20 @@
     lows = jnp.concatenate([low, low], axis=1)
     patches = SPLIT // 2
 
+    left_ref, back_left_ref, range_ref, back_range_ref = (
+        table_ref.at[rows, columns] for rows, columns in (
+            (pl.ds(0, LANES), pl.ds(0, LANES)), (pl.ds(0, LANES), pl.ds(LANES, LANES)),
+            (pl.ds(LANES, LANES), pl.ds(0, LANES)), (pl.ds(LANES, PATCH), pl.ds(LANES, LANES)),
+        )
+    )
+    wide = 2 * LANES
+    starts = np.cumsum([wide, wide, wide, 4 * wide, 2 * wide, 2 * wide]).tolist()
+    right_ref, back_right_ref, look_ref, azimuth_one_ref, azimuth_two_ref, back_azimuth_ref = (
+        table_ref.at[pl.ds(start, rows)]
+        for start, rows in zip(starts, (wide, wide, 4 * wide, 2 * wide, 2 * wide, 2 * wide))
+    )
+    tc_ref, ts_ref = twiddle_ref.at[pl.ds(0, SPLIT)], twiddle_ref.at[pl.ds(SPLIT, SPLIT)]
+
     barrier = pltpu.get_barrier_semaphore()
 
     def greet(o, carry):
@@ -214,85 +227,93 @@
         return carry
 
     lax.fori_loop(1, scene, greet, 0)
-    for load in loads:
+    for load in slabs + loads:
         load.start()
-    loads[0].wait()
-    height = packed_ref.shape[0]
-    piece = height // 8
-
-    def spread(i, carry):
-        rows = pl.ds(pl.multiple_of(i * piece, piece), piece)
-        spread_ref[rows] = packed_ref[rows].astype(jnp.float32)
-        return carry
-
-    lax.fori_loop(0, 8, spread, 0)
+    piece = packed_ref.shape[0] // (2 * SLABS)
+    for n, slab in enumerate(slabs):
+        slab.wait()
+        for half in range(2):
+            rows = pl.ds((2 * n + half) * piece, piece)
+            spread_ref[rows] = packed_ref[rows].astype(jnp.float32)
     owners = LANES // STRIP
     tiles = scene // owners
     stride = 2 * tiles * dates
 
-    def turn(d):
-        def body(tile, carry):
-            for c in range(2):
-                start = (c * tiles + tile) * dates + d
-                bins = spread_ref[pl.ds(start, lines_held, stride=stride)].T
-                for n in range(owners):
-                    own = bins[n * STRIP : (n + 1) * STRIP]
-                    rim = jnp.concatenate([own[:SHIFT], own[STRIP - SHIFT :]], axis=0)
-                    core = own[SHIFT : STRIP - SHIFT]
-                    raw_ref[d, 0, tile * owners + n, c] = rim.astype(jnp.bfloat16)
-                    raw_ref[d, 1, tile * owners + n, c] = core.astype(jnp.bfloat16)
+    def piece_of(ref, k, owner):
+        return ref.at[k // 2, k % 2, owner]
+
+    def strip_copy(k, peer):
+        return pltpu.make_async_remote_copy(
+            src_ref=piece_of(raw_ref, k, peer),
+            dst_ref=piece_of(recv_ref, k, me),
+            send_sem=send_sem.at[k],
+            recv_sem=recv_sem.at[k],
+            device_id={"scene": peer},
+            device_id_type=pl.DeviceIdType.MESH,
+        )
+
+    def own_copy(k):
+        return pltpu.make_async_copy(
+            piece_of(raw_ref, k, me), piece_of(recv_ref, k, me), recv_sem.at[k]
+        )
+
+    def turn(d, tile):
+        for c in range(2):
+            start = (c * tiles + tile) * dates + d
+            bins = spread_ref[pl.ds(start, lines_held, stride=stride)].T
+            for n in range(owners):
+                own = bins[n * STRIP : (n + 1) * STRIP]
+                rim = jnp.concatenate([own[:SHIFT], own[STRIP - SHIFT :]], axis=0)
+                core = own[SHIFT : STRIP - SHIFT]
+                raw_ref[d, 0, tile * owners + n, c] = rim.astype(jnp.bfloat16)
+                raw_ref[d, 1, tile * owners + n, c] = core.astype(jnp.bfloat16)
+
+    def turn_and_send(d):
+        def body(i, carry):
+            tile = lax.rem(me // owners + tiles // 2 + i, tiles)
+            turn(d, tile)
+
+            @pl.when(i == 0)
+            def _():
+                if d == 0:
+                    pl.semaphore_wait(barrier, scene - 1)
+
+            for n in range(owners):
+                peer = tile * owners + n
+
+                @pl.when(peer != me)
+                def _():
+                    strip_copy(2 * d, peer).start()
+
             return carry
 
         lax.fori_loop(0, tiles, body, 0)
-
-    turn(0)
-    pl.semaphore_wait(barrier, scene - 1)
+        own_copy(2 * d).start()
 
     def far(i):
         half = (i + 1) // 2
         return scene // 2 + half * (1 - 2 * lax.rem(i, 2))
 
-    def piece_of(ref, k, owner):
-        return ref.at[k // 2, k % 2, owner]
-
-    def strip_copy(k, o):
-        peer = lax.rem(me + o, scene)
-        return pltpu.make_async_remote_copy(
-            src_ref=piece_of(raw_ref, k, peer),
-            dst_ref=piece_of(recv_ref, k, me),
-            send_sem=send_sem.at[k, o],
-            recv_sem=recv_sem.at[k, o],
-            device_id={"scene": peer},
-            device_id_type=pl.DeviceIdType.MESH,
-        )
-
-    def own_copy(k):
-        return pltpu.make_async_copy(
-            piece_of(raw_ref, k, me), piece_of(recv_ref, k, me), local_sem.at[k]
-        )
-
     def send_all(k):
         def send(i, carry):
-            strip_copy(k, far(i)).start()
+            strip_copy(k, lax.rem(me + far(i), scene)).start()
             return carry
 
         lax.fori_loop(0, scene - 1, send, 0)
         own_copy(k).start()
 
     def arrive_all(k):
-        def arrive(o, carry):
-            strip_copy(k, o).wait_recv()
-            return carry
-
-        lax.fori_loop(1, scene, arrive, 0)
-        own_copy(k).wait()
-
-    send_all(0)
-    for d in range(1, dates):
-        turn(d)
-        send_all(2 * d)
-
-    for load in loads[1:]:
+        held = recv_ref.at[k // 2, k % 2]
+        pltpu.make_async_copy(held, held, recv_sem.at[k]).wait()
+
+    def sent_all(k):
+        held = raw_ref.at[k // 2, k % 2, pl.ds(0, scene - 1)]
+        pltpu.make_async_copy(held, held, send_sem.at[k]).wait()
+
+    for d in range(dates):
+        turn_and_send(d)
+
+    for load in loads:
         load.wait()
 
     for part in range(SPLIT // 2):
@@ -338,11 +359,11 @@
         return (
             neighbour(
                 own_ref.at[HALO_CHUNKS + big], own_before_ref.at[big],
-                look_send.at[big, 0], look_recv.at[big, 0], 1,
+                look_send.at[0], look_recv.at[0], 1,
             ),
             neighbour(
                 own_ref.at[big], own_after_ref.at[big],
-                look_send.at[big, 1], look_recv.at[big, 1], -1,
+                look_send.at[1], look_recv.at[1], -1,
             ),
         )
 
@@ -387,7 +408,7 @@
             re, im = (mixed[k : k + SPLIT, n * LANES : (n + 1) * LANES] for k in (0, SPLIT))
             segments.append(jnp.concatenate([re * tc + im * ts, im * tc - re * ts], axis=1))
         stacked = jnp.concatenate(segments, axis=0).astype(jnp.bfloat16)
-        spectra = dot(stacked, right_ref[...]) * (1.0 / SPLIT)
+        spectra = dot(stacked, right_ref[...])
         return [spectra[n * SPLIT : (n + 1) * SPLIT] for n in range(count)]
 
     def turned(pair):
@@ -461,7 +482,7 @@
             re, im = rows[:, :LANES], rows[:, LANES:]
             segments.append(jnp.concatenate([re * tc - im * ts, im * tc + re * ts], axis=0))
         stacked = jnp.concatenate(segments, axis=1).astype(jnp.bfloat16)
-        second = (dot(back_left_ref[...], stacked) * (1.0 / SPLIT)).astype(jnp.bfloat16)
+        second = dot(back_left_ref[...], stacked).astype(jnp.bfloat16)
         return [second[:, j * LANES : (j + 1) * LANES] for j in range(4)]
 
     def focus_first(big, carry):
@@ -513,13 +534,13 @@
                     )
                 )
             lines = jnp.concatenate(rows, axis=0).astype(jnp.bfloat16)
-            result = dot(lines, azimuth_ref[...]).astype(jnp.bfloat16).astype(jnp.float32)
+            results = [dot(lines, ref[...]) for ref in (azimuth_one_ref, azimuth_two_ref)]
             for j in range(4):
                 for r in range(4):
                     start = ((first_chunk + 4 * step + j) * 4 + r) * patches
-                    grid_ref[pl.ds(pl.multiple_of(start, patches), patches)] = result[
-                        j * patches : (j + 1) * patches, r * LANES : (r + 1) * LANES
-                    ]
+                    part = results[r // 2][j * patches : (j + 1) * patches]
+                    part = part[:, (r % 2) * LANES : (r % 2 + 1) * LANES]
+                    grid_ref[pl.ds(pl.multiple_of(start, patches), patches)] = part
             return carry
 
         lax.fori_loop(0, count // 4, forward_lines, 0)
@@ -528,15 +549,13 @@
         line_ref[HALO_CHUNKS + j, pl.ds(1, SPLIT)] = own_ref[j].astype(jnp.float32)
     lines_of(HALO_CHUNKS, CHUNKS)
     for k in range(2 * dates):
-
-        def sent(o, carry):
-            strip_copy(k, o).wait_send()
-            return carry
-
-        lax.fori_loop(1, scene, sent, 0)
-
-    for big in range(HALO_CHUNKS):
-        wait_pair(look_copies(big))
+        sent_all(k)
+    wait_pair(
+        (
+            neighbour(own_before_ref, own_before_ref, look_send.at[0], look_recv.at[0], 1),
+            neighbour(own_after_ref, own_after_ref, look_send.at[1], look_recv.at[1], -1),
+        )
+    )
     for j in range(HALO_CHUNKS):
         line_ref[j, pl.ds(1, SPLIT)] = own_before_ref[j].astype(jnp.float32)
         line_ref[HALO_CHUNKS + CHUNKS + j, pl.ds(1, SPLIT)] = own_after_ref[j].astype(jnp.float32)
@@ -553,7 +572,7 @@
             re = jnp.where(low, one, pltpu.roll(two, PATCH, 1))
             im = jnp.where(low, pltpu.roll(one, PATCH, 1), two)
             stacks.append(jnp.concatenate([re, im], axis=0).astype(jnp.bfloat16))
-        spectra = dot(range_ref[...], jnp.concatenate(stacks, axis=1)) * (1.0 / PATCH)
+        spectra = dot(range_ref[...], jnp.concatenate(stacks, axis=1))
         kept_re, kept_im = [], []
         for pair in range(2 * STEPS):
             re = spectra[:PATCH, pair * LANES : (pair + 1) * LANES]
@@ -578,7 +597,7 @@
         for n in range(STEPS):
             rows = back[n * PATCH : (n + 1) * PATCH]
             stacked.append(jnp.concatenate([rows[:, :LANES], rows[:, LANES:]], axis=0))
-        result = dot(back_range_ref[...], jnp.concatenate(stacked, axis=1)) * (1.0 / PATCH)
+        result = dot(back_range_ref[...], jnp.concatenate(stacked, axis=1))
         width = STEPS * LANES
         start = pl.multiple_of(step * width, width)
         out_ref[:, pl.ds(start, width)] = result.astype(jnp.bfloat16)
@@ -587,38 +606,60 @@
     lax.fori_loop(0, patches // (4 * STEPS), filter_patches, 0)
 
 
-def loading_kernel(band_ref, *refs):
+def loading_kernel(*refs):
     held, out_ref, kept, load_sem = refs[:TABLES], refs[TABLES], refs[TABLES + 1 : -1], refs[-1]
+    rows = held[0].shape[0] // SLABS
+    slabs = [
+        pltpu.make_async_copy(
+            held[0].at[pl.ds(n * rows, rows)], kept[0].at[pl.ds(n * rows, rows)], load_sem.at[n]
+        )
+        for n in range(SLABS)
+    ]
     loads = [
-        pltpu.make_async_copy(source, target, load_sem.at[i])
-        for i, (source, target) in enumerate(zip(held, kept[:TABLES]))
+        pltpu.make_async_copy(held[i], kept[i], load_sem.at[SLABS - 1 + i])
+        for i in range(1, TABLES)
     ]
-    scene_kernel(band_ref, *kept[:TABLES], out_ref, *kept[TABLES:], loads)
+    scene_kernel(*kept[:TABLES], out_ref, *kept[TABLES:], slabs, loads)
+
+
+def table_stack(left):
+    unit = 1.0 / SPLIT
+    back_range = np.zeros((LANES, LANES))
+    back_range[:PATCH] = back_range_table() * unit
+    azimuth = patch_azimuth_table()
+    return np.concatenate(
+        [
+            np.concatenate([left, left_table(-1.0) * unit], axis=1),
+            np.concatenate([patch_range_table() * unit, back_range], axis=1),
+            spectrum_side(right_table(1.0), 1) * unit,
+            spectrum_side(right_table(-1.0), 0),
+            look_table(),
+            azimuth[:, : 2 * LANES],
+            azimuth[:, 2 * LANES :],
+            back_azimuth_table(),
+        ]
+    )
 
 
 def run_scene(raw, band, phase, left, scene, shape):
     dates, width = shape[1], shape[3]
     looks = SPLIT * SPLIT // LOOKS
-    tc, ts = twiddle_tables()
     vmem = pl.BlockSpec(memory_space=pltpu.VMEM)
     plane = (GROUPS, SPLIT, LANES)
     edge = pltpu.VMEM((dates, SHIFT, SPLIT, LANES), jnp.bfloat16)
     looked_edge = pltpu.VMEM((HALO_CHUNKS, SPLIT, LANES), jnp.bfloat16)
     dma = pltpu.SemaphoreType.DMA
-    tables = (
-        raw, phase, bf16(left), bf16(spectrum_side(right_table(1.0), 1)),
-        bf16(spectrum_side(right_table(-1.0), 0)), bf16(left_table(-1.0)),
-        jnp.asarray(tc), jnp.asarray(ts), bf16(look_table()),
-        bf16(patch_azimuth_table()), bf16(patch_range_table()),
-        bf16(back_azimuth_table()), bf16(back_range_table()),
-    )
+    twiddles = np.concatenate(twiddle_tables())
+    tables = (raw, band, phase, bf16(table_stack(left)), jnp.asarray(twiddles))
     return pl.pallas_call(
         loading_kernel,
-        in_specs=[pl.BlockSpec(memory_space=pltpu.SMEM)]
-        + [pl.BlockSpec(memory_space=pl.ANY)] * TABLES,
+        in_specs=[pl.BlockSpec(memory_space=pl.ANY)] * TABLES,
         out_specs=vmem,
         out_shape=pltpu.VMEM((2 * STRIP, looks), jnp.bfloat16),
-        scratch_shapes=[pltpu.VMEM(table.shape, table.dtype) for table in tables]
+        scratch_shapes=[
+            (pltpu.SMEM if table is band else pltpu.VMEM)(table.shape, table.dtype)
+            for table in tables
+        ]
         + [
             pltpu.VMEM((dates, 2, scene, 2, HALF, width), jnp.bfloat16),
             pltpu.VMEM(raw.shape, jnp.float32),
@@ -637,15 +678,14 @@
             looked_edge,
             pltpu.VMEM((2 * CHUNKS, SPLIT + 8, LANES), jnp.float32),
             pltpu.VMEM((PATCH * SPLIT // 2, LANES), jnp.float32),
-            dma((2 * dates, scene)), dma((2 * dates, scene)), dma((2 * dates,)),
-            dma((dates, 2)), dma((dates, 2)),
-            dma((HALO_CHUNKS, 2)), dma((HALO_CHUNKS, 2)), dma((TABLES,)),
+            dma((2 * dates,)), dma((2 * dates,)),
+            dma((dates, 2)), dma((dates, 2)), dma((2,)), dma((2,)), dma((SLABS - 1 + TABLES,)),
         ],
         compiler_params=pltpu.CompilerParams(
             vmem_limit_bytes=VMEM_LIMIT, collective_id=0, has_side_effects=True
         ),
         name="scene",
-    )(*[pltpu.with_memory_space_constraint(t, pltpu.HBM) for t in (band, *tables)])
+    )(*[pltpu.with_memory_space_constraint(t, pltpu.HBM) for t in tables])
 
 
 def on_device(raw_echoes, azimuth_phase, band_offset, partners):

time: 43 us -> 40.9 us (0.951)
  Pallas kernels: 42.1 us -> 40.1 us
    pallas_call x1, Pallas kernels: 42.1 us -> 40.1 us  [run_scene(): pl.pallas_call(loading_kernel, in_specs=[pl.BlockSpec(memory_space=pl.ANY...]
where the time goes in v3:
time: 40.9 us; the launch traced here: 40.8 us
  Pallas kernels  40.1 us (98%)
  local copies, waits for them, and re-layouts  0.73 us (2%)
    pallas_call x1, Pallas kernels, run_scene(): pl.pallas_call(loading_kernel, in_specs=[pl.BlockSpec(memory_space=pl.ANY...  40.1 us

profile of v3, /device:TPU:1, one launch (start us, length us, event | category | flops | bytes accessed | tf_op | source)
XLA Modules:
  0.0 40.8 jit_solution(12261441019905131917)
XLA Ops:
  0.0 40.1 %scene.1 = bf16[64,1024]{1,0:T(8,128)(2,1)S(1)} custom-call(bf16[4096,128]{1,0:T(8,128)(2,1)} %bitcast.10, s32[32]{0:T(128)} %refs_1_.1, f32[32,4096]{1,0:T(8,128)} %bitcast.11, bf16[3328,256]{1,0:T(8,128)(2,1)} %constant.4.clone.refs_3_, f32[128,128]{1,0:T(8,128)} %constant.5.clone.refs_4_), custom_call_target="tpu_custom_call" | custom-call | tf_op jit(solution)/shard_map/scene/pallas_call | solution.py:654
  40.1 0.7 %broadcast_bitcast_fusion = bf16[2,1024,2,32]{1,3,2,0:T(8,128)(2,1)} fusion(bf16[2,32,1024]{2,1,0:T(8,128)(2,1)S(1)} %bitcast.9), kind=kLoop, calls=%fused_computation | loop fusion | bytes 393216 | tf_op jit(solution)/shard_map/transpose | solution.py:707

commit v4 on v3

--- a/solution.py
+++ b/solution.py
@@ -21,7 +21,7 @@
 HALO_CHUNKS = CHUNKS // 2
 HALF = STRIP // 2
 BATCH = 8
-STEPS = 4
+STEPS = 8
 TABLES = 5
 SLABS = 4
 VMEM_LIMIT = 40 * 1024 * 1024
@@ -512,10 +512,11 @@
         return carry
 
     send_all(1)
-    for d in range(dates):
-        arrive_all(2 * d)
-        forward_rim(d)
+    arrive_all(0)
+    forward_rim(0)
+    arrive_all(2)
     send_all(3)
+    forward_rim(1)
     arrive_all(1)
     forward_core(0)
     lax.fori_loop(0, GROUPS // 4, focus_first, 0, unroll=2)
@@ -523,31 +524,23 @@
     forward_core(1)
     lax.fori_loop(0, GROUPS // 8, focus_last, 0)
 
-    def lines_of(first_chunk, count):
-        def forward_lines(step, carry):
-            rows = []
-            for j in range(4):
-                chunk = first_chunk + 4 * step + j
-                rows.append(
-                    jnp.concatenate(
-                        [line_ref[chunk, pl.ds(p, patches, stride=2)] for p in range(4)], axis=1
-                    )
-                )
-            lines = jnp.concatenate(rows, axis=0).astype(jnp.bfloat16)
-            results = [dot(lines, ref[...]) for ref in (azimuth_one_ref, azimuth_two_ref)]
-            for j in range(4):
+    def lines_of(*firsts):
+        rows = []
+        for chunk in (first + j for first in firsts for j in range(HALO_CHUNKS)):
+            parts = [line_ref[chunk, pl.ds(p, patches, stride=2)] for p in range(4)]
+            rows.append(jnp.concatenate(parts, axis=1))
+        lines = jnp.concatenate(rows, axis=0).astype(jnp.bfloat16)
+        results = [dot(lines, ref[...]) for ref in (azimuth_one_ref, azimuth_two_ref)]
+        for n, first in enumerate(firsts):
+            for j in range(HALO_CHUNKS):
                 for r in range(4):
-                    start = ((first_chunk + 4 * step + j) * 4 + r) * patches
-                    part = results[r // 2][j * patches : (j + 1) * patches]
+                    part = results[r // 2][(n * HALO_CHUNKS + j) * patches :][:patches]
                     part = part[:, (r % 2) * LANES : (r % 2 + 1) * LANES]
-                    grid_ref[pl.ds(pl.multiple_of(start, patches), patches)] = part
-            return carry
-
-        lax.fori_loop(0, count // 4, forward_lines, 0)
+                    grid_ref[pl.ds(((first + j) * 4 + r) * patches, patches)] = part
 
     for j in range(CHUNKS):
         line_ref[HALO_CHUNKS + j, pl.ds(1, SPLIT)] = own_ref[j].astype(jnp.float32)
-    lines_of(HALO_CHUNKS, CHUNKS)
+    lines_of(HALO_CHUNKS, 2 * HALO_CHUNKS)
     for k in range(2 * dates):
         sent_all(k)
     wait_pair(
@@ -559,8 +552,7 @@
     for j in range(HALO_CHUNKS):
         line_ref[j, pl.ds(1, SPLIT)] = own_before_ref[j].astype(jnp.float32)
         line_ref[HALO_CHUNKS + CHUNKS + j, pl.ds(1, SPLIT)] = own_after_ref[j].astype(jnp.float32)
-    lines_of(0, HALO_CHUNKS)
-    lines_of(HALO_CHUNKS + CHUNKS, HALO_CHUNKS)
+    lines_of(0, HALO_CHUNKS + CHUNKS)
     lane = lax.broadcasted_iota(jnp.int32, (PATCH, LANES), 1)
     opening, closing = lane % PATCH == 0, lane % PATCH == PATCH - 1
 
@@ -577,7 +569,8 @@
         for pair in range(2 * STEPS):
             re = spectra[:PATCH, pair * LANES : (pair + 1) * LANES]
             im = spectra[PATCH:, pair * LANES : (pair + 1) * LANES]
-            magnitude = jnp.sqrt(re * re + im * im + EPSILON)
+            power = re * re + im * im + EPSILON
+            magnitude = power * lax.rsqrt(power)
             rows = magnitude + pltpu.roll(magnitude, 1, 0) + pltpu.roll(magnitude, PATCH - 1, 0)
             left = jnp.where(opening, pltpu.roll(rows, PATCH + 1, 1), pltpu.roll(rows, 1, 1))
             right = jnp.where(closing, pltpu.roll(rows, PATCH - 1, 1), pltpu.roll(rows, LANES - 1, 1))
@@ -603,7 +596,7 @@
         out_ref[:, pl.ds(start, width)] = result.astype(jnp.bfloat16)
         return carry
 
-    lax.fori_loop(0, patches // (4 * STEPS), filter_patches, 0)
+    lax.fori_loop(0, patches // (4 * STEPS), filter_patches, 0, unroll=1)
 
 
 def loading_kernel(*refs):

time: 40.9 us -> 39.2 us (0.958)
  Pallas kernels: 40.1 us -> 38.3 us
    pallas_call x1, Pallas kernels: 40.1 us -> 38.3 us  [run_scene(): pl.pallas_call(loading_kernel, in_specs=[pl.BlockSpec(memory_space=pl.ANY...]
where the time goes in v4:
time: 39.2 us; the launch traced here: 39 us
  Pallas kernels  38.3 us (98%)
  local copies, waits for them, and re-layouts  0.73 us (2%)
    pallas_call x1, Pallas kernels, run_scene(): pl.pallas_call(loading_kernel, in_specs=[pl.BlockSpec(memory_space=pl.ANY...  38.3 us

profile of v4, /device:TPU:1, one launch (start us, length us, event | category | flops | bytes accessed | tf_op | source)
XLA Modules:
  0.0 39.0 jit_solution(12575507851997800698)
XLA Ops:
  0.0 38.3 %scene.1 = bf16[64,1024]{1,0:T(8,128)(2,1)S(1)} custom-call(bf16[4096,128]{1,0:T(8,128)(2,1)} %bitcast.10, s32[32]{0:T(128)} %refs_1_.1, f32[32,4096]{1,0:T(8,128)} %bitcast.11, bf16[3328,256]{1,0:T(8,128)(2,1)} %constant.4.clone.refs_3_, f32[128,128]{1,0:T(8,128)} %constant.5.clone.refs_4_), custom_call_target="tpu_custom_call" | custom-call | tf_op jit(solution)/shard_map/scene/pallas_call | solution.py:647
  38.3 0.7 %broadcast_bitcast_fusion = bf16[2,1024,2,32]{1,3,2,0:T(8,128)(2,1)} fusion(bf16[2,32,1024]{2,1,0:T(8,128)(2,1)S(1)} %bitcast.9), kind=kLoop, calls=%fused_computation | loop fusion | bytes 393216 | tf_op jit(solution)/shard_map/transpose | solution.py:700

commit v5 on v4

--- a/solution.py
+++ b/solution.py
@@ -20,7 +20,8 @@
 CHUNKS = STRIP // 4
 HALO_CHUNKS = CHUNKS // 2
 HALF = STRIP // 2
-BATCH = 8
+HALF_LANES = 32
+UPS, DOWNS = SHIFT - 2, SHIFT - 3
 STEPS = 8
 TABLES = 5
 SLABS = 4
@@ -90,6 +91,14 @@
     return np.block([[c, s], [-s, c]])
 
 
+def smooth_table():
+    k = np.arange(PATCH)
+    gap = (k[:, None] - k[None, :]) % PATCH
+    near = ((gap <= 1) | (gap == PATCH - 1)).astype(np.float64)
+    eye = np.eye(2)
+    return np.concatenate([np.kron(eye, near), np.kron(eye, np.ones((PATCH, PATCH)))], axis=1)
+
+
 def back_azimuth_table():
     c, s = base_tables()
     c, s = c[:, 16:48], s[:, 16:48]
@@ -113,8 +122,11 @@
 
 
 def lane_order():
-    lane = np.arange(SPLIT)
-    return 2 * (lane % (SPLIT // 2)) + lane // (SPLIT // 2)
+    quarter = SPLIT // 4
+    places = np.arange(SPLIT // 2)
+    fast = places[quarter // 2 : 3 * quarter // 2]
+    slow = np.concatenate([places[: quarter // 2], places[3 * quarter // 2 :]])
+    return np.concatenate([2 * fast, 2 * fast + 1, 2 * slow, 2 * slow + 1])
 
 
 def spectrum_side(table, axis):
@@ -139,8 +151,11 @@
     shape = (SPLIT, LANES)
     lane = lax.broadcasted_iota(jnp.int32, shape, 1)
     row = lax.broadcasted_iota(jnp.int32, shape, 0)
-    half = SPLIT // 2
-    k = row + SPLIT * (2 * (lane & (half - 1)) + ((lane & half) // half))
+    quarter = SPLIT // 4
+    place, odd = lane & (quarter - 1), (lane & quarter) // quarter
+    slow = jnp.where(place < quarter // 2, place, place + quarter)
+    place = jnp.where((lane & (2 * quarter)) != 0, slow, place + quarter // 2)
+    k = row + SPLIT * (2 * place + odd)
     total = SPLIT * SPLIT
     f = jnp.where(k < total // 2, k, k - total).astype(jnp.float32)
     ratio = f * (2.0 / total)
@@ -168,7 +183,13 @@
         weight_ref[g, tap] = jnp.concatenate([weight, weight], axis=1).astype(jnp.bfloat16)
     first = lines_ref[pl.ds(g, SPLIT // 2, stride=STRIP)]
     second = lines_ref[pl.ds(g + GROUPS, SPLIT // 2, stride=STRIP)]
-    pieces = [first, pltpu.roll(first, SPLIT, 1), second, pltpu.roll(second, SPLIT, 1)]
+    cuts = (0, quarter // 2, 3 * quarter // 2, SPLIT // 2)
+    pieces = []
+    for even in (first, second):
+        both = (even, pltpu.roll(even, SPLIT, 1))
+        thirds = [[part[a:b] for a, b in zip(cuts, cuts[1:])] for part in both]
+        pieces += [thirds[0][1], thirds[1][1]]
+        pieces += [thirds[0][0], thirds[0][2], thirds[1][0], thirds[1][2]]
     angle = jnp.concatenate(pieces, axis=0).T[:SPLIT]
     cos_ref[g], sin_ref[g] = cos_sin(angle)
 
@@ -201,6 +222,7 @@
     local = lines_held // SPLIT
     low = lax.broadcasted_iota(jnp.int32, (SPLIT, LANES), 1) < SPLIT
     lows = jnp.concatenate([low, low], axis=1)
+    fast = lax.broadcasted_iota(jnp.int32, (SPLIT, LANES), 1) % SPLIT < HALF_LANES
     patches = SPLIT // 2
 
     left_ref, back_left_ref, range_ref, back_range_ref = (
@@ -210,10 +232,13 @@
         )
     )
     wide = 2 * LANES
-    starts = np.cumsum([wide, wide, wide, 4 * wide, 2 * wide, 2 * wide]).tolist()
-    right_ref, back_right_ref, look_ref, azimuth_one_ref, azimuth_two_ref, back_azimuth_ref = (
+    starts = np.cumsum([wide, wide, wide, 4 * wide, 2 * wide, 2 * wide, 2 * wide]).tolist()
+    (
+        right_ref, back_right_ref, look_ref, azimuth_one_ref, azimuth_two_ref,
+        back_azimuth_ref, smooth_ref,
+    ) = (
         table_ref.at[pl.ds(start, rows)]
-        for start, rows in zip(starts, (wide, wide, 4 * wide, 2 * wide, 2 * wide, 2 * wide))
+        for start, rows in zip(starts, (wide, wide, 4 * wide, 2 * wide, 2 * wide, 2 * wide, LANES))
     )
     tc_ref, ts_ref = twiddle_ref.at[pl.ds(0, SPLIT)], twiddle_ref.at[pl.ds(SPLIT, SPLIT)]
 
@@ -346,12 +371,10 @@
     def edge_copies(d):
         return (
             neighbour(
-                up_ref.at[d, pl.ds(1, SHIFT - 1)], before_ref.at[d, pl.ds(1, SHIFT - 1)],
-                edge_send.at[d, 0], edge_recv.at[d, 0], 1,
+                up_ref.at[d], before_ref.at[d], edge_send.at[d, 0], edge_recv.at[d, 0], 1,
             ),
             neighbour(
-                down_ref.at[d, pl.ds(0, SHIFT - 1)], after_ref.at[d, pl.ds(0, SHIFT - 1)],
-                edge_send.at[d, 1], edge_recv.at[d, 1], -1,
+                down_ref.at[d], after_ref.at[d], edge_send.at[d, 1], edge_recv.at[d, 1], -1,
             ),
         )
 
@@ -418,39 +441,42 @@
     def forward_rim(d):
         widen(d, 0)
 
-        def body(step, carry):
-            for n, rim in enumerate(transform(BATCH * step, BATCH)):
-                i = BATCH * step + n
-                flipped = turned(rim)
-                rim_ref[d, i] = rim
-                down = jnp.where(low, rim[:, :LANES], flipped[:, LANES:])
-                up = jnp.where(low, flipped[:, :LANES], rim[:, LANES:])
-                down_ref[d, i] = down.astype(jnp.bfloat16)
-                up_ref[d, i] = up.astype(jnp.bfloat16)
-            return carry
-
-        lax.fori_loop(0, SHIFT // BATCH, body, 0, unroll=True)
+        ups, downs = [], []
+        for i, rim in enumerate(transform(0, SHIFT)):
+            flipped = turned(rim)
+            rim_ref[d, i] = rim
+            downs.append(jnp.where(low, rim[:, :LANES], flipped[:, LANES:]))
+            ups.append(jnp.where(low, flipped[:, :LANES], rim[:, LANES:]))
+        ups = [jnp.where(fast, pltpu.roll(ups[2], LANES - HALF_LANES, 1), ups[1])] + ups[3:]
+        downs = downs[:3] + [
+            jnp.where(fast, downs[i], pltpu.roll(downs[i + 1], HALF_LANES, 1)) for i in (3, 5)
+        ]
+        for n, up in enumerate(ups):
+            up_ref[d, n] = up.astype(jnp.bfloat16)
+        for n, down in enumerate(downs):
+            down_ref[d, n] = down.astype(jnp.bfloat16)
         start_pair(edge_copies(d))
 
     def forward_core(d):
         widen(d, 1)
         wait_pair(edge_copies(d))
 
-        def body(step, carry):
-            for n, core in enumerate(transform(BATCH * step, BATCH)):
-                i = BATCH * step + n
-                before = before_ref[d, i].astype(jnp.float32)
-                after = after_ref[d, i].astype(jnp.float32)
-                before = jnp.concatenate([before, pltpu.roll(before, SPLIT, 1)], axis=1)
-                after = jnp.concatenate([pltpu.roll(after, SPLIT, 1), after], axis=1)
-                rim, flipped = rim_ref[d, i], turned(core)
-                ext_ref[i] = jnp.where(lows, before, flipped).astype(jnp.bfloat16)
-                ext_ref[SHIFT + i] = jnp.where(lows, rim, core).astype(jnp.bfloat16)
-                ext_ref[2 * SHIFT + i] = jnp.where(lows, core, rim).astype(jnp.bfloat16)
-                ext_ref[3 * SHIFT + i] = jnp.where(lows, flipped, after).astype(jnp.bfloat16)
-            return carry
-
-        lax.fori_loop(0, SHIFT // BATCH, body, 0, unroll=True)
+        befores = [before_ref[d, n].astype(jnp.float32) for n in range(UPS)]
+        befores = [befores[0], befores[0], pltpu.roll(befores[0], HALF_LANES, 1)] + befores[1:]
+        afters = [after_ref[d, n].astype(jnp.float32) for n in range(DOWNS)]
+        afters = afters[:3] + [
+            part for after in afters[3:]
+            for part in (after, pltpu.roll(after, LANES - HALF_LANES, 1))
+        ]
+        afters.append(afters[-1])
+        for i, core in enumerate(transform(0, SHIFT)):
+            before = jnp.concatenate([befores[i], pltpu.roll(befores[i], SPLIT, 1)], axis=1)
+            after = jnp.concatenate([pltpu.roll(afters[i], SPLIT, 1), afters[i]], axis=1)
+            rim, flipped = rim_ref[d, i], turned(core)
+            ext_ref[i] = jnp.where(lows, before, flipped).astype(jnp.bfloat16)
+            ext_ref[SHIFT + i] = jnp.where(lows, rim, core).astype(jnp.bfloat16)
+            ext_ref[2 * SHIFT + i] = jnp.where(lows, core, rim).astype(jnp.bfloat16)
+            ext_ref[3 * SHIFT + i] = jnp.where(lows, flipped, after).astype(jnp.bfloat16)
 
     def migrate(big):
         totals = [[] for _ in range(4)]
@@ -553,9 +579,6 @@
         line_ref[j, pl.ds(1, SPLIT)] = own_before_ref[j].astype(jnp.float32)
         line_ref[HALO_CHUNKS + CHUNKS + j, pl.ds(1, SPLIT)] = own_after_ref[j].astype(jnp.float32)
     lines_of(0, HALO_CHUNKS + CHUNKS)
-    lane = lax.broadcasted_iota(jnp.int32, (PATCH, LANES), 1)
-    opening, closing = lane % PATCH == 0, lane % PATCH == PATCH - 1
-
     def filter_patches(step, carry):
         stacks = []
         for pair in range(2 * STEPS):
@@ -565,20 +588,22 @@
             im = jnp.where(low, pltpu.roll(one, PATCH, 1), two)
             stacks.append(jnp.concatenate([re, im], axis=0).astype(jnp.bfloat16))
         spectra = dot(range_ref[...], jnp.concatenate(stacks, axis=1))
-        kept_re, kept_im = [], []
+        parts, sums = [], []
         for pair in range(2 * STEPS):
             re = spectra[:PATCH, pair * LANES : (pair + 1) * LANES]
             im = spectra[PATCH:, pair * LANES : (pair + 1) * LANES]
             power = re * re + im * im + EPSILON
             magnitude = power * lax.rsqrt(power)
             rows = magnitude + pltpu.roll(magnitude, 1, 0) + pltpu.roll(magnitude, PATCH - 1, 0)
-            left = jnp.where(opening, pltpu.roll(rows, PATCH + 1, 1), pltpu.roll(rows, 1, 1))
-            right = jnp.where(closing, pltpu.roll(rows, PATCH - 1, 1), pltpu.roll(rows, LANES - 1, 1))
-            column = jnp.sum(magnitude, axis=0, keepdims=True)
-            first = jnp.sum(jnp.where(low[:1], column, 0.0), axis=1, keepdims=True)
-            second = jnp.sum(jnp.where(low[:1], 0.0, column), axis=1, keepdims=True)
-            level = jnp.where(low[:1], first, second) * (1.0 / (PATCH * PATCH)) + EPSILON
-            gain = (rows + left + right) * ((1.0 / 9.0) / level)
+            parts.append((re, im))
+            sums.append(rows.astype(jnp.bfloat16))
+        boxes = dot(jnp.concatenate(sums, axis=0), smooth_ref[...])
+        kept_re, kept_im = [], []
+        for pair, (re, im) in enumerate(parts):
+            box = boxes[pair * PATCH : (pair + 1) * PATCH]
+            total = jnp.sum(box[:, LANES:], axis=0, keepdims=True)
+            level = total * (1.0 / (3 * PATCH * PATCH)) + EPSILON
+            gain = box[:, :LANES] * ((1.0 / 9.0) / level)
             kept_re.append((re * gain).astype(jnp.bfloat16))
             kept_im.append((im * gain).astype(jnp.bfloat16))
         kept = [
@@ -630,6 +655,7 @@
             azimuth[:, : 2 * LANES],
             azimuth[:, 2 * LANES :],
             back_azimuth_table(),
+            smooth_table(),
         ]
     )
 
@@ -639,7 +665,7 @@
     looks = SPLIT * SPLIT // LOOKS
     vmem = pl.BlockSpec(memory_space=pltpu.VMEM)
     plane = (GROUPS, SPLIT, LANES)
-    edge = pltpu.VMEM((dates, SHIFT, SPLIT, LANES), jnp.bfloat16)
+    ups, downs = (pltpu.VMEM((dates, n, SPLIT, LANES), jnp.bfloat16) for n in (UPS, DOWNS))
     looked_edge = pltpu.VMEM((HALO_CHUNKS, SPLIT, LANES), jnp.bfloat16)
     dma = pltpu.SemaphoreType.DMA
     twiddles = np.concatenate(twiddle_tables())
@@ -664,7 +690,7 @@
             pltpu.VMEM(plane, jnp.float32),
             pltpu.VMEM((GROUPS + 2 * SHIFT, SPLIT, 2 * LANES), jnp.bfloat16),
             pltpu.VMEM((dates, SHIFT, SPLIT, 2 * LANES), jnp.float32),
-            edge, edge, edge, edge,
+            ups, downs, ups, downs,
             pltpu.VMEM((GROUPS, 2 * SPLIT, LANES), jnp.bfloat16),
             pltpu.VMEM((CHUNKS, SPLIT, LANES), jnp.bfloat16),
             looked_edge,

time: 39.2 us -> 38.7 us (0.987)
  Pallas kernels: 38.3 us -> 37.8 us
    pallas_call x1, Pallas kernels: 38.3 us -> 37.8 us  [run_scene(): pl.pallas_call(loading_kernel, in_specs=[pl.BlockSpec(memory_space=pl.ANY...]
where the time goes in v5:
time: 38.7 us; the launch traced here: 38.5 us
  Pallas kernels  37.8 us (98%)
  local copies, waits for them, and re-layouts  0.73 us (2%)
    pallas_call x1, Pallas kernels, run_scene(): pl.pallas_call(loading_kernel, in_specs=[pl.BlockSpec(memory_space=pl.ANY...  37.8 us

profile of v5, /device:TPU:1, one launch (start us, length us, event | category | flops | bytes accessed | tf_op | source)
XLA Modules:
  0.0 38.5 jit_solution(18221166602108395337)
XLA Ops:
  0.0 37.8 %scene.1 = bf16[64,1024]{1,0:T(8,128)(2,1)S(1)} custom-call(bf16[4096,128]{1,0:T(8,128)(2,1)} %bitcast.10, s32[32]{0:T(128)} %refs_1_.1, f32[32,4096]{1,0:T(8,128)} %bitcast.11, bf16[3456,256]{1,0:T(8,128)(2,1)} %constant.4.clone.refs_3_, f32[128,128]{1,0:T(8,128)} %constant.5.clone.refs_4_), custom_call_target="tpu_custom_call" | custom-call | tf_op jit(solution)/shard_map/scene/pallas_call | solution.py:673
  37.8 0.7 %broadcast_bitcast_fusion = bf16[2,1024,2,32]{1,3,2,0:T(8,128)(2,1)} fusion(bf16[2,32,1024]{2,1,0:T(8,128)(2,1)S(1)} %bitcast.9), kind=kLoop, calls=%fused_computation | loop fusion | bytes 393216 | tf_op jit(solution)/shard_map/transpose | solution.py:726

commit v6 on v5

--- a/solution.py
+++ b/solution.py
@@ -493,42 +493,41 @@
                 totals[j].append(sums[0] + sums[1])
         return [jnp.concatenate(total, axis=0) for total in totals]
 
-    def focus(big):
+    def focus(step):
         compressed = []
-        for j, migrated in enumerate(migrate(big)):
-            re, im = migrated[:, :LANES], migrated[:, LANES:]
-            cos_phase, sin_phase = cos_ref[4 * big + j], sin_ref[4 * big + j]
-            parts = [re * cos_phase - im * sin_phase, im * cos_phase + re * sin_phase]
-            compressed.append(jnp.concatenate(parts, axis=1).astype(jnp.bfloat16))
+        for big in range(2):
+            for j, migrated in enumerate(migrate(2 * step + big)):
+                g = 8 * step + 4 * big + j
+                re, im = migrated[:, :LANES], migrated[:, LANES:]
+                cos_phase, sin_phase = cos_ref[g], sin_ref[g]
+                parts = [re * cos_phase - im * sin_phase, im * cos_phase + re * sin_phase]
+                compressed.append(jnp.concatenate(parts, axis=1).astype(jnp.bfloat16))
         first = dot(jnp.concatenate(compressed, axis=0), back_right_ref[...])
         tc, ts = tc_ref[...], ts_ref[...]
         segments = []
-        for j in range(4):
+        for j in range(8):
             rows = first[j * SPLIT : (j + 1) * SPLIT]
             re, im = rows[:, :LANES], rows[:, LANES:]
             segments.append(jnp.concatenate([re * tc - im * ts, im * tc + re * ts], axis=0))
         stacked = jnp.concatenate(segments, axis=1).astype(jnp.bfloat16)
         second = dot(back_left_ref[...], stacked).astype(jnp.bfloat16)
-        return [second[:, j * LANES : (j + 1) * LANES] for j in range(4)]
-
-    def focus_first(big, carry):
-        for j, focused in enumerate(focus(big)):
-            focused_ref[4 * big + j] = focused
+        return [second[:, j * LANES : (j + 1) * LANES] for j in range(8)]
+
+    def focus_first(step, carry):
+        for j, focused in enumerate(focus(step)):
+            focused_ref[8 * step + j] = focused
         return carry
 
     def focus_last(step, carry):
-        products = []
-        for n in range(2):
-            big = 2 * step + n
-            pieces = []
-            for j, focused in enumerate(focus(big)):
-                leading = focused.astype(jnp.float32)
-                trailing = focused_ref[4 * big + j].astype(jnp.float32)
-                lr, li = leading[:SPLIT], leading[SPLIT:]
-                tr, ti = trailing[:SPLIT], trailing[SPLIT:]
-                product = jnp.concatenate([lr * tr + li * ti, li * tr - lr * ti], axis=1)
-                pieces.append(product.astype(jnp.bfloat16))
-            products.append(jnp.concatenate(pieces, axis=1))
+        pieces = []
+        for j, focused in enumerate(focus(step)):
+            leading = focused.astype(jnp.float32)
+            trailing = focused_ref[8 * step + j].astype(jnp.float32)
+            lr, li = leading[:SPLIT], leading[SPLIT:]
+            tr, ti = trailing[:SPLIT], trailing[SPLIT:]
+            product = jnp.concatenate([lr * tr + li * ti, li * tr - lr * ti], axis=1)
+            pieces.append(product.astype(jnp.bfloat16))
+        products = [jnp.concatenate(pieces[4 * n : 4 * n + 4], axis=1) for n in range(2)]
         looked = dot(jnp.concatenate(products, axis=0), look_ref[...]).astype(jnp.bfloat16)
         for n in range(2):
             big, rows = 2 * step + n, slice(n * SPLIT, (n + 1) * SPLIT)
@@ -545,7 +544,7 @@
     forward_rim(1)
     arrive_all(1)
     forward_core(0)
-    lax.fori_loop(0, GROUPS // 4, focus_first, 0, unroll=2)
+    lax.fori_loop(0, GROUPS // 8, focus_first, 0)
     arrive_all(3)
     forward_core(1)
     lax.fori_loop(0, GROUPS // 8, focus_last, 0)

time: 38.7 us -> 38.6 us (level)
  no operation moved by 1% of the time
where the time goes in v6:
time: 38.6 us; the launch traced here: 38.4 us
  Pallas kernels  37.6 us (97%)
  local copies, waits for them, and re-layouts  0.73 us (2%)
    pallas_call x1, Pallas kernels, run_scene(): pl.pallas_call(loading_kernel, in_specs=[pl.BlockSpec(memory_space=pl.ANY...  37.6 us

profile of v6, /device:TPU:1, one launch (start us, length us, event | category | flops | bytes accessed | tf_op | source)
XLA Modules:
  0.0 38.4 jit_solution(775777145913787605)
XLA Ops:
  0.0 37.6 %scene.1 = bf16[64,1024]{1,0:T(8,128)(2,1)S(1)} custom-call(bf16[4096,128]{1,0:T(8,128)(2,1)} %bitcast.10, s32[32]{0:T(128)} %refs_1_.1, f32[32,4096]{1,0:T(8,128)} %bitcast.11, bf16[3456,256]{1,0:T(8,128)(2,1)} %constant.4.clone.refs_3_, f32[128,128]{1,0:T(8,128)} %constant.5.clone.refs_4_), custom_call_target="tpu_custom_call" | custom-call | tf_op jit(solution)/shard_map/scene/pallas_call | solution.py:672
  37.6 0.7 %broadcast_bitcast_fusion = bf16[2,1024,2,32]{1,3,2,0:T(8,128)(2,1)} fusion(bf16[2,32,1024]{2,1,0:T(8,128)(2,1)S(1)} %bitcast.9), kind=kLoop, calls=%fused_computation | loop fusion | bytes 393216 | tf_op jit(solution)/shard_map/transpose | solution.py:725

commit v7 on v6

--- a/solution.py
+++ b/solution.py
@@ -242,6 +242,8 @@
     )
     tc_ref, ts_ref = twiddle_ref.at[pl.ds(0, SPLIT)], twiddle_ref.at[pl.ds(SPLIT, SPLIT)]
 
+    for slab in slabs:
+        slab.start()
     barrier = pltpu.get_barrier_semaphore()
 
     def greet(o, carry):
@@ -251,15 +253,15 @@
         )
         return carry
 
-    lax.fori_loop(1, scene, greet, 0)
-    for load in slabs + loads:
-        load.start()
+    lax.fori_loop(1, scene, greet, 0, unroll=True)
     piece = packed_ref.shape[0] // (2 * SLABS)
     for n, slab in enumerate(slabs):
         slab.wait()
         for half in range(2):
             rows = pl.ds((2 * n + half) * piece, piece)
             spread_ref[rows] = packed_ref[rows].astype(jnp.float32)
+    for load in loads:
+        load.start()
     owners = LANES // STRIP
     tiles = scene // owners
     stride = 2 * tiles * dates

time: 38.6 us -> 38.6 us (level)
  no operation moved by 1% of the time
where the time goes in v7:
time: 38.6 us; the launch traced here: 38.4 us
  Pallas kernels  37.6 us (97%)
  local copies, waits for them, and re-layouts  0.73 us (2%)
    pallas_call x1, Pallas kernels, run_scene(): pl.pallas_call(loading_kernel, in_specs=[pl.BlockSpec(memory_space=pl.ANY...  37.6 us

profile of v7, /device:TPU:1, one launch (start us, length us, event | category | flops | bytes accessed | tf_op | source)
XLA Modules:
  0.0 38.4 jit_solution(6225683929037671163)
XLA Ops:
  0.0 37.6 %scene.1 = bf16[64,1024]{1,0:T(8,128)(2,1)S(1)} custom-call(bf16[4096,128]{1,0:T(8,128)(2,1)} %bitcast.10, s32[32]{0:T(128)} %refs_1_.1, f32[32,4096]{1,0:T(8,128)} %bitcast.11, bf16[3456,256]{1,0:T(8,128)(2,1)} %constant.4.clone.refs_3_, f32[128,128]{1,0:T(8,128)} %constant.5.clone.refs_4_), custom_call_target="tpu_custom_call" | custom-call | tf_op jit(solution)/shard_map/scene/pallas_call | solution.py:674
  37.6 0.7 %broadcast_bitcast_fusion = bf16[2,1024,2,32]{1,3,2,0:T(8,128)(2,1)} fusion(bf16[2,32,1024]{2,1,0:T(8,128)(2,1)S(1)} %bitcast.9), kind=kLoop, calls=%fused_computation | loop fusion | bytes 393216 | tf_op jit(solution)/shard_map/transpose | solution.py:727

commit v8 on v7

--- a/solution.py
+++ b/solution.py
@@ -210,7 +210,7 @@
     packed_ref, band_ref, phase_ref, table_ref, twiddle_ref,
     out_ref,
     raw_ref, spread_ref, recv_ref, lines_ref, wide_ref, weight_ref, cos_ref, sin_ref, ext_ref,
-    rim_ref, up_ref, down_ref, before_ref, after_ref, focused_ref,
+    rim_ref, core_ref, up_ref, down_ref, before_ref, after_ref, focused_ref,
     own_ref, own_before_ref, own_after_ref, line_ref, grid_ref,
     send_sem, recv_sem, edge_send, edge_recv, look_send, look_recv,
     slabs, loads,
@@ -461,8 +461,11 @@
 
     def forward_core(d):
         widen(d, 1)
+        if d == 0:
+            for i, core in enumerate(transform(0, SHIFT)):
+                core_ref[i] = core
         wait_pair(edge_copies(d))
-
+        cores = [core_ref[i] for i in range(SHIFT)] if d == 0 else transform(0, SHIFT)
         befores = [before_ref[d, n].astype(jnp.float32) for n in range(UPS)]
         befores = [befores[0], befores[0], pltpu.roll(befores[0], HALF_LANES, 1)] + befores[1:]
         afters = [after_ref[d, n].astype(jnp.float32) for n in range(DOWNS)]
@@ -471,7 +474,7 @@
             for part in (after, pltpu.roll(after, LANES - HALF_LANES, 1))
         ]
         afters.append(afters[-1])
-        for i, core in enumerate(transform(0, SHIFT)):
+        for i, core in enumerate(cores):
             before = jnp.concatenate([befores[i], pltpu.roll(befores[i], SPLIT, 1)], axis=1)
             after = jnp.concatenate([pltpu.roll(afters[i], SPLIT, 1), afters[i]], axis=1)
             rim, flipped = rim_ref[d, i], turned(core)
@@ -541,8 +544,8 @@
     send_all(1)
     arrive_all(0)
     forward_rim(0)
+    send_all(3)
     arrive_all(2)
-    send_all(3)
     forward_rim(1)
     arrive_all(1)
     forward_core(0)
@@ -691,6 +694,7 @@
             pltpu.VMEM(plane, jnp.float32),
             pltpu.VMEM((GROUPS + 2 * SHIFT, SPLIT, 2 * LANES), jnp.bfloat16),
             pltpu.VMEM((dates, SHIFT, SPLIT, 2 * LANES), jnp.float32),
+            pltpu.VMEM((SHIFT, SPLIT, 2 * LANES), jnp.float32),
             ups, downs, ups, downs,
             pltpu.VMEM((GROUPS, 2 * SPLIT, LANES), jnp.bfloat16),
             pltpu.VMEM((CHUNKS, SPLIT, LANES), jnp.bfloat16),

time: 38.6 us -> 38.6 us (level)
  no operation moved by 1% of the time
where the time goes in v8:
time: 38.6 us; the launch traced here: 38.4 us
  Pallas kernels  37.6 us (97%)
  local copies, waits for them, and re-layouts  0.73 us (2%)
    pallas_call x1, Pallas kernels, run_scene(): pl.pallas_call(loading_kernel, in_specs=[pl.BlockSpec(memory_space=pl.ANY...  37.6 us

profile of v8, /device:TPU:1, one launch (start us, length us, event | category | flops | bytes accessed | tf_op | source)
XLA Modules:
  0.0 38.4 jit_solution(4515131328091163091)
XLA Ops:
  0.0 37.6 %scene.1 = bf16[64,1024]{1,0:T(8,128)(2,1)S(1)} custom-call(bf16[4096,128]{1,0:T(8,128)(2,1)} %bitcast.10, s32[32]{0:T(128)} %refs_1_.1, f32[32,4096]{1,0:T(8,128)} %bitcast.11, bf16[3456,256]{1,0:T(8,128)(2,1)} %constant.4.clone.refs_3_, f32[128,128]{1,0:T(8,128)} %constant.5.clone.refs_4_), custom_call_target="tpu_custom_call" | custom-call | tf_op jit(solution)/shard_map/scene/pallas_call | solution.py:677
  37.7 0.7 %broadcast_bitcast_fusion = bf16[2,1024,2,32]{1,3,2,0:T(8,128)(2,1)} fusion(bf16[2,32,1024]{2,1,0:T(8,128)(2,1)S(1)} %bitcast.9), kind=kLoop, calls=%fused_computation | loop fusion | bytes 393216 | tf_op jit(solution)/shard_map/transpose | solution.py:731
